TPU v7x, 32 devices: a whole 2x2x4 slice. The times are simulated.
32 devices in a mesh: tm: 4 (over z), feat: 8 (over y, x, core).
Axes of the slice: x: 2, y: 2, z: 4, core: 2. Of those that a mesh axis runs over, the one named last changes fastest.
Arguments:
- trajectory: float32 [16384, 2048], P('tm', 'feat'), may hold values from -8 to 9
Outputs:
- moments: float32 [4, 2048, 2048], P(None, 'feat', 'tm')
All inputs are finite; a program needn't handle non-finite values.
Results may differ from a plain program's by a relative error of at most 0.00035.
Values may be sent and summed in bfloat16 or wider, within the bound.
No kernel may reach another device: no remote copies, remote signals or barrier semaphores. Data moves between devices by JAX's collectives and lax.ppermute only.
A program may use at most 128 MiB of HBM per device.

v0:
```python
import jax
import jax.numpy as jnp
from jax import lax
from jax.sharding import PartitionSpec as P

HALO = 16


lag_values = (0, 1, 4, 16)


def passed_along(value, axis, steps):
    count = lax.axis_size(axis)
    initial, last = (max(0, -steps), min(count, count - steps))
    return lax.ppermute(value, axis, [(source, source + steps) for source in range(initial, last)])


def shards(trajectory):
    rows = trajectory.shape[0]
    frames = rows * lax.axis_size("tm")
    total = lax.psum(jnp.sum(trajectory, axis=0), "tm")
    mean = total / frames
    centered = (trajectory - mean).astype(jnp.bfloat16)
    gathered = lax.all_gather(centered, "feat", axis=1, tiled=True)
    tail = passed_along(gathered[:HALO], "tm", -1)
    extended = jnp.concatenate([gathered, tail], axis=0)
    blocks = [
        lax.dot_general(
            centered,
            extended[lag : lag + rows],
            (((0,), (0,)), ((), ())),
            preferred_element_type=jnp.float32,
        )
        for lag in lag_values
    ]
    partial_sum = jnp.stack(blocks)
    summed = lax.psum_scatter(partial_sum, "tm", scatter_dimension=2, tiled=True)
    scales = jnp.sqrt(jnp.float32(frames) - jnp.array(lag_values, jnp.float32))
    return summed / scales[:, None, None]


def solution(mesh):
    placed = (P("tm", "feat"),)
    return jax.shard_map(
        shards, mesh=mesh, in_specs=placed, out_specs=P(None, "feat", "tm"), check_vma=False
    )
```

profile of v0, /device:TPU:0, one launch (start us, length us, event | category | flops | bytes accessed | tf_op | source)
XLA Modules:
  0.0 323.2 jit_solution(11681123390294850944)
XLA Ops:
  6.5 0.0 all-gather.2.cloned.1.call-start
  6.5 2.7 reduce_sum.9
  9.3 13.5 %psum.7 = f32[256]{0:T(256)S(1)} all-reduce(f32[256]{0:T(256)S(1)} %reduce_sum.9), channel_id=1, replica_groups=mesh['tm'=4,'feat'=8] {'tm'}, use_global_device_ids=true, to_apply=%region_1.0 | all-reduce | flops 256 | bytes 2048 | tf_op jit(solution)/shard_map/psum | solution.py:21
  22.8 3.9 %subtract_convert_fusion = bf16[4096,256]{1,0:T(8,128)(2,1)} fusion(f32[4096,256]{1,0:T(8,128)} %param.2, f32[256]{0:T(256)S(1)} %broadcast_multiply_fusion.1), kind=kLoop, calls=%fused_computation.7 | loop fusion | flops 2097152 | bytes 6292480 | tf_op jit(solution)/shard_map/convert_element_type | solution.py:23
  26.6 0.0 all-gather.2.cloned.1.call-update
  26.7 0.0 reduce-scatter.2.cloned.1.call-start
  26.7 91.3 %all-gather.2.cloned.1.call-done = bf16[4096,2048]{1,0:T(8,128)(2,1)} async-done(((bf16[4096,256]{1,0:T(8,128)(2,1)}), bf16[4096,2048]{1,0:T(8,128)(2,1)}) %all-gather.2.cloned.1.call-update) | async-done | bytes 16777232 | tf_op jit(solution)/shard_map/all_gather | solution.py:24
  118.0 0.8 slice.16
  118.9 1.3 collective-permute-start
  120.2 0.0 copy-start
  120.2 8.9 %convolution_bitcast_fusion = f32[1,256,2048]{2,1,0:T(8,128)S(1)} fusion(bf16[4096,256]{1,0:T(8,128)(2,1)} %subtract_convert_fusion, bf16[4096,2048]{1,0:T(8,128)(2,1)} %all-gather.2.cloned.1.call-done), kind=kOutput, calls=%fused_computation.11 | convolution fusion | flops 4294967296 | bytes 20971520 | tf_op jit(solution)/shard_map/dot_general | solution.py:28
  129.1 2.2 copy-done
  131.3 0.0 copy-start.1
  131.3 7.0 %constant_dynamic-update-slice_fusion.1 = bf16[4112,2048]{1,0:T(8,128)(2,1)} fusion(bf16[4096,2048]{1,0:T(8,128)(2,1)S(1)} %copy-done), kind=kLoop, calls=%fused_computation.14 | loop fusion | bytes 33554432
  138.3 0.0 collective-permute-done
  138.3 0.6 constant_dynamic-update-slice_fusion
  138.9 0.0 copy-done.1
  138.9 8.2 %fusion.12 = f32[1,256,2048]{2,1,0:T(8,128)S(1)} fusion(bf16[4096,256]{1,0:T(8,128)(2,1)S(1)} %copy-done.1, bf16[4112,2048]{1,0:T(8,128)(2,1)} %constant_dynamic-update-slice_fusion), kind=kOutput, calls=%fused_computation.10 | convolution fusion | flops 4294967296 | bytes 20971520 | tf_op jit(solution)/shard_map/dot_general | solution.py:28
  147.1 8.2 %fusion.9 = f32[1,256,2048]{2,1,0:T(8,128)S(1)} fusion(bf16[4096,256]{1,0:T(8,128)(2,1)S(1)} %copy-done.1, bf16[4112,2048]{1,0:T(8,128)(2,1)} %constant_dynamic-update-slice_fusion), kind=kOutput, calls=%fused_computation.9 | convolution fusion | flops 4294967296 | bytes 20971520 | tf_op jit(solution)/shard_map/dot_general | solution.py:28
  155.3 8.2 %fusion.6 = f32[1,256,2048]{2,1,0:T(8,128)S(1)} fusion(bf16[4096,256]{1,0:T(8,128)(2,1)S(1)} %copy-done.1, bf16[4112,2048]{1,0:T(8,128)(2,1)} %constant_dynamic-update-slice_fusion), kind=kOutput, calls=%fused_computation.8 | convolution fusion | flops 4294967296 | bytes 20971520 | tf_op jit(solution)/shard_map/dot_general | solution.py:28
  163.5 3.7 %pad_maximum_fusion = f32[4,256,2048]{2,1,0:T(8,128)} fusion(f32[1,256,2048]{2,1,0:T(8,128)S(1)} %fusion.12, f32[1,256,2048]{2,1,0:T(8,128)S(1)} %fusion.9, f32[1,256,2048]{2,1,0:T(8,128)S(1)} %fusion.6, f32[1,256,2048]{2,1,0:T(8,128)S(1)} %convolution_bitcast_fusion), kind=kLoop, calls=%fused_computation.6 | loop fusion | flops 6291456 | bytes 16777216 | tf_op jit(solution)/shard_map/stack | solution.py:36
  167.2 0.0 copy-start.2
  167.2 0.0 reduce-scatter.2.cloned.1.call-update
  167.2 145.9 %reduce-scatter.2.cloned.1.call-done = f32[4,256,512]{2,1,0:T(8,128)} async-done(((f32[4,256,2048]{2,1,0:T(8,128)}), f32[4,256,512]{2,1,0:T(8,128)}) %reduce-scatter.2.cloned.1.call-update) | async-done | bytes 2097168 | tf_op jit(solution)/shard_map/reduce_scatter | solution.py:37
  313.1 0.0 copy-done.2
  313.1 3.3 %broadcast_multiply_fusion = f32[4,256,512]{2,1,0:T(8,128)} fusion(f32[4,256,512]{2,1,0:T(8,128)} %reduce-scatter.2.cloned.1.call-done, f32[4]{0:T(128)S(1)} %copy-done.2), kind=kLoop, calls=%fused_computation.12 | loop fusion | flops 524288 | bytes 4194320 | tf_op jit(solution)/shard_map/div | solution.py:39
  (1 shorter events, 0.0 us)
Async XLA Ops:
  6.5 111.5 %all-gather.2.cloned.1.call-start = ((), (), s32[]{:S(2)}) async-start(), calls=%async_computation.1 | async-start | bytes 18874368 | tf_op jit(solution)/shard_map/all_gather | solution.py:24
  26.7 286.4 %reduce-scatter.2.cloned.1.call-start = ((), (), s32[]{:S(2)}) async-start(), calls=%async_computation.2 | async-start | bytes 10485760 | tf_op jit(solution)/shard_map/reduce_scatter | solution.py:37
  118.9 19.4 %collective-permute-start = (bf16[16,2048]{1,0:T(8,128)(2,1)S(1)}, bf16[16,2048]{1,0:T(8,128)(2,1)S(1)}, u32[]{:S(2)}, u32[]{:S(2)}) collective-permute-start(bf16[16,2048]{1,0:T(8,128)(2,1)S(1)} %slice.16), channel_id=1, source_target_pairs={{8,0},{16,8},{24,16},{9,1},{17,9},{25,17},{10,2},{18,10},{26,18},{... | collective-permute-start | bytes 196616 | tf_op jit(solution)/shard_map/ppermute | solution.py:15
  120.2 11.1 %copy-start = (bf16[4096,2048]{1,0:T(8,128)(2,1)S(1)}, bf16[4096,2048]{1,0:T(8,128)(2,1)}, u32[]{:S(2)}) copy-start(bf16[4096,2048]{1,0:T(8,128)(2,1)} %all-gather.2.cloned.1.call-done) | copy-start | bytes 50331652
  131.3 7.6 %copy-start.1 = (bf16[4096,256]{1,0:T(8,128)(2,1)S(1)}, bf16[4096,256]{1,0:T(8,128)(2,1)}, u32[]{:S(2)}) copy-start(bf16[4096,256]{1,0:T(8,128)(2,1)} %subtract_convert_fusion) | copy-start | bytes 6291460
  167.2 145.9 %copy-start.2 = (f32[4]{0:T(128)S(1)}, f32[4]{0:T(128)}, u32[]{:S(2)}) copy-start(f32[4]{0:T(128)} %constant.13) | copy-start | bytes 52
Sparse Core Ops, SparseCore 0:
  26.8 91.2 all-gather.1
  167.3 145.7 reduce-scatter.1
where the time goes:
time: 324 us; the launch traced here: 323 us
  waiting for transfers between devices  237 us (73%)
  matrix products  33.5 us (10%)
  other arithmetic  13.5 us (4%)
  blocking collectives  13.5 us (4%)
  between operations  13.5 us (4%)
  local copies, waits for them, and re-layouts  10.7 us (3%)
    reduce_scatter x1, waiting for transfers between devices, shards(): lax.psum_scatter(partial_sum, 'tm', scatter_dimension=2, tiled=True)  146 us
    all_gather x1, waiting for transfers between devices, shards(): gathered = lax.all_gather(centered, 'feat', axis=1, tiled=True)  91.3 us
    dot_general x4, matrix products, shards(): lax.dot_general(centered, extended[lag:lag + rows], (((0,), (0,)), ((), (...  33.5 us
    psum x1, blocking collectives, shards(): total = lax.psum(jnp.sum(trajectory, axis=0), 'tm')  13.5 us
    unnamed x7, local copies, waits for them, and re-layouts  9.21 us
  transfers between devices with their start and end apart: 3, of which 2 were waited for; matrix products, arithmetic and copies ran while one was open for 5% of the time, Pallas kernels for 0%

commit v1 on v0

v1 whole, which is shorter than its diff:
```python
import math

import jax
import jax.numpy as jnp
from jax import lax
from jax.experimental import pallas as pl
from jax.experimental.pallas import tpu as pltpu
from jax.sharding import PartitionSpec as P


LAGS = (0, 1, 4, 16)
HALO = max(LAGS)


def bits(mask):
    return [b for b in range(mask.bit_length()) if mask >> b & 1]


def last_hop(mask, half):
    return bits(mask)[-1] if half == 0 else bits(mask)[0]


def arrivals(chips):
    singles = [m for m in range(1, chips) if len(bits(m)) == 1]
    order = [(m, i % 2) for i, m in enumerate(singles)]
    order += [(m, 1 - i % 2) for i, m in enumerate(singles)]
    if len(singles) % 2:
        order = [(m, h) for m in singles for h in (0, 1)]
    several = [m for m in range(1, chips) if len(bits(m)) > 1]
    order += [(m, h) for m in sorted(several, key=lambda m: len(bits(m))) for h in (0, 1)]
    return [order[i : i + 2] for i in range(0, len(order), 2)]


def tree_levels(q, count):
    def rep(low, size):
        if low <= q < low + size:
            return q
        return low + size - 1 if low + size <= q else low

    levels, size = [], 2
    while size <= count:
        moves = []
        for low in range(0, count, size):
            target = rep(low, size)
            a, b = rep(low, size // 2), rep(low + size // 2, size // 2)
            moves.append((a if target == b else b, target))
        levels.append(moves)
        size *= 2
    return levels


def lagged_kernel(own_ref, own_next_ref, other_ref, other_next_ref, out_ref, wide_ref, exact_ref):
    rows, cols = own_ref.shape
    for i, (ref, after) in enumerate(((own_ref, own_next_ref), (other_ref, other_next_ref))):
        exact_ref[:rows] = ref[...]
        exact_ref[rows:] = after[...]
        wide_ref[:rows] = ref[...].astype(jnp.float32)
        wide_ref[rows:] = after[...].astype(jnp.float32)
        for k, lag in enumerate(LAGS):
            start = HALO - lag
            source = exact_ref if start % 16 == 0 else wide_ref
            at = (len(LAGS) * i + k) * cols
            out_ref[:, at : at + cols] = source[start : start + rows].astype(out_ref.dtype)


def lagged_columns(own, other):
    rows, cols = own.shape[0] - HALO, own.shape[1]
    step = math.gcd(rows, 512)
    main = pl.BlockSpec((step, cols), lambda i: (i, 0))
    after = pl.BlockSpec((HALO, cols), lambda i: ((i + 1) * (step // HALO), 0))
    wide = 2 * len(LAGS) * cols

    def body(own_ref, own_next_ref, other_ref, other_next_ref, out_ref, wide_ref, exact_ref):
        rows_here = pl.ds(pl.multiple_of(pl.program_id(0) * step, step), step)
        lagged_kernel(
            own_ref, own_next_ref, other_ref, other_next_ref, out_ref.at[rows_here], wide_ref, exact_ref
        )

    return pl.pallas_call(
        body,
        out_shape=pltpu.VMEM((rows, wide), own.dtype),
        grid=(rows // step,),
        in_specs=[main, after, main, after],
        out_specs=pl.BlockSpec(memory_space=pltpu.VMEM),
        scratch_shapes=[
            pltpu.VMEM((step + HALO, cols), jnp.float32),
            pltpu.VMEM((step + HALO, cols), own.dtype),
        ],
        cost_estimate=pl.CostEstimate(
            flops=rows * wide, bytes_accessed=2 * rows * (wide + 2 * cols), transcendentals=0
        ),
        compiler_params=pltpu.CompilerParams(vmem_limit_bytes=16 * 1024 * 1024),
        name="lagged",
    )(own, own, other, other)


def make(mesh):
    nz, nf = mesh.shape["tm"], mesh.shape["feat"]
    chips = nf // 2
    levels = nz.bit_length() - 1

    def shards(trajectory):
        rows, cols = trajectory.shape
        half = cols // 2
        tall = len(LAGS) * cols
        frames = rows * nz
        z, f = lax.axis_index("tm"), lax.axis_index("feat")
        chip, core = lax.div(f, 2), lax.rem(f, 2)
        mine = lax.bitwise_xor(chip, z)
        room = 2.0 ** math.floor(math.log2(32768.0 / frames))

        def hop(mask):
            return [(i, i ^ mask) for i in range(nf)]

        stats = jnp.stack([jnp.sum(trajectory, 0), jnp.max(trajectory, 0), jnp.min(trajectory, 0)])
        others = [
            lax.ppermute(stats, "tm", [(i, (i + k) % nz) for i in range(nz)])
            for k in range(1, nz)
        ]
        total, high, low = stats
        for other in others:
            total = total + other[0]
            high, low = jnp.maximum(high, other[1]), jnp.minimum(low, other[2])
        mean = total / frames
        spread = high - low + jnp.maximum(jnp.abs(high), jnp.abs(low)) * 2.0**-14
        power = jnp.ceil(jnp.log2(jnp.maximum(spread, 2.0**-60)))
        shrink = lax.reduce_precision(jnp.exp2(-power), 8, 7)
        grow = lax.reduce_precision(jnp.exp2(power), 8, 7)

        def centre(value, low=0, high=cols):
            return ((value - mean[low:high]) * shrink[low:high]).astype(jnp.bfloat16)

        got = {}
        for h in (0, 1):
            low, high = h * half, (h + 1) * half
            got[0, h] = centre(trajectory[:, low:high], low, high)
            mean, shrink, got[0, h] = lax.optimization_barrier((mean, shrink, got[0, h]))
        slots = arrivals(chips)
        for slot in slots:
            for m, h in slot:
                if len(bits(m)) == 1:
                    got[m, h] = lax.ppermute(got[0, h], "feat", hop(2 * m))

        before = lax.ppermute(trajectory[rows - HALO :], "tm", [(i, i + 1) for i in range(nz - 1)])
        first = jnp.where(z == 0, jnp.bfloat16(0), centre(before))
        own = jnp.concatenate([first, jnp.concatenate([got[0, 0], got[0, 1]], 1)])
        lagged = lagged_columns(own, lax.ppermute(own, "feat", hop(1)))

        turned = lax.ppermute(grow[None], "feat", hop(1))[0]
        pair = jnp.stack([jnp.where(core == 0, grow, turned), jnp.where(core == 0, turned, grow)])
        across = pair
        for m in range(1, chips):
            across = jnp.where(mine == m, lax.ppermute(pair, "feat", hop(2 * m)), across)

        def product(blocks, low=0, high=2 * tall):
            value = lax.dot_general(
                lagged[:, low:high],
                jnp.concatenate(blocks, 1) if len(blocks) > 1 else blocks[0],
                (((0,), (0,)), ((), ())),
                preferred_element_type=jnp.float32,
            )
            return (value * room).astype(jnp.float16)

        def wide(value):
            return value.astype(jnp.float32)

        def rise(mask, level, flip=0):
            return [
                (x * nf + j, y * nf + (j ^ flip))
                for j in range(nf)
                for x, y in tree_levels(j // 2 ^ mask, nz)[level]
            ]

        both = ("tm", "feat")
        top = levels - 1
        none = jnp.float32(0)

        def add(values):
            total = wide(values[0])
            for value in values[1:]:
                total = total + wide(value)
            return total

        def climbed(part, mask, until):
            terms = [part]
            for level in range(until):
                sent = part if level == 0 else add(terms).astype(jnp.float16)
                terms.append(lax.ppermute(sent, both, rise(mask, level)))
            return terms

        part = product([own[HALO:]])
        terms = climbed(part, 0, top)
        terms.append(lax.ppermute(add(terms).astype(jnp.float16), both, rise(0, top)))
        kept = [[(0, [v[:, h * half : (h + 1) * half] for v in terms])] for h in (0, 1)]

        for slot in slots:
            for m, h in slot:
                if len(bits(m)) > 1:
                    axis = 1 << last_hop(m, h)
                    got[m, h] = lax.ppermute(got[m ^ axis, h], "feat", hop(2 * axis))

        late = [[], []]
        for s, slot in enumerate(slots):
            (a, ha), (b, hb) = slot
            blocks = [got[u] for u in slot]
            if a != b:
                if s == 0:
                    part = product(blocks)
                else:
                    part = jnp.concatenate(
                        [product(blocks, i * tall, (i + 1) * tall) for i in (0, 1)]
                    )
                sides = [
                    climbed(part[:, i * half : (i + 1) * half], m, top)
                    for i, (m, _) in enumerate(slot)
                ]
                pairs = rise(a, top) + rise(b, top)
                assert all(len({p[i] for p in pairs}) == len(pairs) for i in (0, 1))
                sender = sum(
                    jnp.where(lax.bitwise_xor(chip, a) == q, tree_levels(q, nz)[top][0][0], 0)
                    for q in range(nz)
                )
                sent = jnp.where(z == sender, *map(add, sides)).astype(jnp.float16)
                back = lax.ppermute(sent, both, pairs)
                kept[ha].append((a, sides[0] + [back]))
                kept[hb].append((b, sides[1] + [back]))
                continue
            sums = []
            for i in (0, 1):
                part = product(blocks, i * tall, (i + 1) * tall)
                terms = climbed(part, a, top)
                sent = add(terms).astype(jnp.float16)
                late[i].append(lax.ppermute(sent, both, rise(a, top, i)))
                sums.append(terms)
            kept[ha].append((a, [[v[:, :half] for v in terms] for terms in sums]))
            kept[hb].append((b, [[v[:, half:] for v in terms] for terms in sums]))

        sides = []
        for i in (0, 1):
            columns = []
            for h in (0, 1):
                total = none
                for m, terms in kept[h]:
                    if isinstance(terms[0], list):
                        terms = terms[i]
                    else:
                        terms = [v[i * tall : (i + 1) * tall] for v in terms]
                    total = jnp.where(mine == m, add(terms), total)
                columns.append(total)
            sides.append(jnp.concatenate(columns, 1))
        near, theirs = sides[0], lax.ppermute(sides[1], "feat", hop(1))

        scales = 1 / (jnp.sqrt(jnp.float32(frames) - jnp.array(LAGS, jnp.float32)) * room)
        out = jnp.zeros((len(LAGS), cols, 2 * cols), jnp.float32)
        for value, added, owner in ((near, late[0], core), (theirs, late[1], 1 - core)):
            for more in added:
                value = value + wide(more)
            value = value.reshape(len(LAGS), cols, cols) * scales[:, None, None]
            value = value * grow[None, :, None] * jnp.where(owner == 0, across[0], across[1])
            out = lax.dynamic_update_slice(out, value, (0, 0, owner * cols))
        return out

    return shards


def plain(trajectory):
    rows = trajectory.shape[0]
    frames = rows * lax.axis_size("tm")
    mean = lax.psum(jnp.sum(trajectory, axis=0), "tm") / frames
    centered = (trajectory - mean).astype(jnp.bfloat16)
    gathered = lax.all_gather(centered, "feat", axis=1, tiled=True)
    steps = [(i, i - 1) for i in range(1, lax.axis_size("tm"))]
    tail = lax.ppermute(gathered[:HALO], "tm", steps)
    extended = jnp.concatenate([gathered, tail], axis=0)
    blocks = [
        lax.dot_general(
            centered,
            extended[lag : lag + rows],
            (((0,), (0,)), ((), ())),
            preferred_element_type=jnp.float32,
        )
        for lag in LAGS
    ]
    summed = lax.psum_scatter(jnp.stack(blocks), "tm", scatter_dimension=2, tiled=True)
    scales = jnp.sqrt(jnp.float32(frames) - jnp.array(LAGS, jnp.float32))
    return summed / scales[:, None, None]


def solution(mesh):
    nz, nf = mesh.shape["tm"], mesh.shape["feat"]
    paired = nf == 2 * nz and nz & (nz - 1) == 0 and nz > 2
    body = make(mesh) if paired else plain

    return jax.shard_map(
        body,
        mesh=mesh,
        in_specs=(P("tm", "feat"),),
        out_specs=P(None, "feat", "tm"),
        check_vma=False,
    )
```

time: 324 us -> 221 us (0.68)
  the two profiles are of different devices: /device:TPU:0 before, /device:TPU:6 now
where the time goes in v1:
time: 221 us
  waiting for transfers between devices  140 us (63%)
  starting transfers between devices  37.5 us (17%)
  matrix products  19.8 us (9%)
  other arithmetic  15.3 us (7%)
  local copies, waits for them, and re-layouts  4.49 us (2%)
  Pallas kernels  3.24 us (1%)
    ppermute x7, waiting for transfers between devices, climbed(): terms.append(lax.ppermute(sent, both, rise(mask, level)))  45.1 us
    ppermute x2, waiting for transfers between devices, shards(): late[i].append(lax.ppermute(sent, both, rise(a, top, i)))  29.8 us
    ppermute x4, waiting for transfers between devices, shards(): got[m, h] = lax.ppermute(got[0, h], 'feat', hop(2 * m))  23.7 us
    ppermute x3, waiting for transfers between devices, shards(): lax.ppermute(pair, 'feat', hop(2 * m))  20.8 us
    ppermute x2, waiting for transfers between devices, shards(): got[m, h] = lax.ppermute(got[m ^ axis, h], 'feat', hop(2 * axis))  20.4 us
    dot_general x6, matrix products, product(): lax.dot_general(lagged[:, low:high], jnp.concatenate(blocks, 1) if len(bl...  19.8 us
    ppermute x7, starting transfers between devices, climbed(): terms.append(lax.ppermute(sent, both, rise(mask, level)))  16 us
    ppermute x3, starting transfers between devices, shards(): lax.ppermute(stats, 'tm', [(i, (i + k) % nz) for i in range(nz)])  5.57 us
  transfers between devices with their start and end apart: 28, of which 10 were waited for; matrix products, arithmetic and copies ran while one was open for 9% of the time, Pallas kernels for 0%

profile of v1, /device:TPU:6, one launch (start us, length us, event | category | flops | bytes accessed | tf_op | source)
XLA Modules:
  0.0 220.8 jit_solution(18301488382908243272)
XLA Ops:
  0.0 2.7 %fusion.52 = (f32[256]{0:T(256)S(1)}, f32[256]{0:T(256)S(1)}, f32[256]{0:T(256)S(1)}) fusion(f32[4096,256]{1,0:T(8,128)} %param.2), kind=kLoop, calls=%fused_computation.81 | loop fusion | flops 3144960 | bytes 4197376 | tf_op jit(solution)/shard_map/reduce_sum | solution.py:115
  2.8 1.6 collective-permute-start.1
  4.4 2.6 %collective-permute-start.2 = (f32[3,256]{1,0:T(4,128)S(1)}, f32[3,256]{1,0:T(4,128)S(1)}, u32[]{:S(2)}, u32[]{:S(2)}) collective-permute-start(f32[3,256]{1,0:T(4,128)S(1)} %pad_maximum_fusion.3), channel_id=1, source_target_pairs={{0,16},{8,24},{16,0},{24,8},{1,17},{9,25},{17,1},{25,9},{2,18},{10... | collective-permute-start | bytes 9224 | tf_op jit(solution)/shard_map/ppermute | solution.py:117
  7.0 1.3 collective-permute-start.3
  8.3 0.7 slice.230
  9.1 2.6 %collective-permute-start = (f32[16,256]{1,0:T(8,128)S(1)}, f32[16,256]{1,0:T(8,128)S(1)}, u32[]{:S(2)}, u32[]{:S(2)}) collective-permute-start(f32[16,256]{1,0:T(8,128)S(1)} %slice.230), channel_id=1, source_target_pairs={{0,8},{8,16},{16,24},{1,9},{9,17},{17,25},{2,10},{10,18},{18,26},{... | collective-permute-start | bytes 49160 | tf_op jit(solution)/shard_map/ppermute | solution.py:144
  11.8 1.8 multiply_convert_fusion.1
  13.7 1.8 multiply_convert_fusion
  16.3 1.6 collective-permute-start.22
  18.4 1.5 collective-permute-start.24
  20.2 0.8 collective-permute-done.22
  21.5 19.9 %collective-permute-done.23 = f32[2,256]{1,0:T(2,128)S(1)} collective-permute-done((f32[2,256]{1,0:T(2,128)S(1)}, f32[2,256]{1,0:T(2,128)S(1)}, u32[]{:S(2)}, u32[]{:S(2)}) %collective-permute-start.23) | collective-permute-done | bytes 2080 | tf_op jit(solution)/shard_map/ppermute | solution.py:153
  42.8 3.8 %collective-permute-done.5 = bf16[4096,128]{1,0:T(8,128)(2,1)S(1)} collective-permute-done((bf16[4096,128]{1,0:T(8,128)(2,1)S(1)}, bf16[4096,128]{1,0:T(8,128)(2,1)S(1)}, u32[]{:S(2)}, u32[]{:S(2)}) %collective-permute-start.5) | collective-permute-done | bytes 1048608 | tf_op jit(solution)/shard_map/ppermute | solution.py:142
  46.6 2.0 collective-permute-start.6
  49.2 19.9 %collective-permute-done.10 = bf16[4096,128]{1,0:T(8,128)(2,1)S(1)} collective-permute-done((bf16[4096,128]{1,0:T(8,128)(2,1)S(1)}, bf16[4096,128]{1,0:T(8,128)(2,1)S(1)}, u32[]{:S(2)}, u32[]{:S(2)}) %collective-permute-start.10) | collective-permute-done | bytes 1048608 | tf_op jit(solution)/shard_map/ppermute | solution.py:142
  69.5 19.4 %collective-permute-done.6 = bf16[4096,128]{1,0:T(8,128)(2,1)S(1)} collective-permute-done((bf16[4096,128]{1,0:T(8,128)(2,1)S(1)}, bf16[4096,128]{1,0:T(8,128)(2,1)S(1)}, u32[]{:S(2)}, u32[]{:S(2)}) %collective-permute-start.6) | collective-permute-done | bytes 1048608 | tf_op jit(solution)/shard_map/ppermute | solution.py:200
  89.1 1.0 collective-permute-done.8
  90.4 3.2 %lagged.1 = bf16[4096,2048]{1,0:T(8,128)(2,1)S(1)} custom-call(bf16[4112,256]{1,0:T(8,128)(2,1)S(1)} %pad_maximum_fusion.own_ref.own_next_ref, bf16[4112,256]{1,0:T(8,128)(2,1)S(1)} %pad_maximum_fusion.own_ref.own_next_ref, bf16[4112,256]{1,0:T(8,128)(2,1)S(1)} %collective-permute-done.4.other_ref.other_next_ref, ...), custom_call_target="tpu_custom_call" | custom-call | flops 8388608 | bytes 20971520 | tf_op jit(solution)/shard_map/lagged/pallas_call | solution.py:79
  93.6 2.4 %fusion.28 = f16[1024,256]{0,1:T(8,128)(2,1)S(1)} fusion(bf16[4096,256]{1,0:T(8,128)(2,1)S(1)} %constant_dynamic-update-slice_fusion.4, bf16[4096,2048]{1,0:T(8,128)(2,1)S(1)} %lagged.1), kind=kOutput, calls=%fused_computation.24 | convolution fusion | flops 2148007936 | bytes 11010048 | tf_op jit(solution)/shard_map/dot_general | solution.py:156
  96.0 2.4 %fusion.31 = f16[1024,256]{0,1:T(8,128)(2,1)S(1)} fusion(bf16[4096,256]{1,0:T(8,128)(2,1)S(1)} %constant_dynamic-update-slice_fusion.4, bf16[4096,2048]{1,0:T(8,128)(2,1)S(1)} %lagged.1), kind=kOutput, calls=%fused_computation.25 | convolution fusion | flops 2148007936 | bytes 11010048 | tf_op jit(solution)/shard_map/dot_general | solution.py:156
  98.4 4.5 %fusion.9 = f16[2048,256]{0,1:T(8,128)(2,1)S(1)} fusion(bf16[4096,2048]{1,0:T(8,128)(2,1)S(1)} %lagged.1, bf16[4096,256]{1,0:T(8,128)(2,1)S(1)} %constant_dynamic-update-slice_fusion), kind=kOutput, calls=%fused_computation.11 | convolution fusion | flops 4296015872 | bytes 19922944 | tf_op jit(solution)/shard_map/dot_general | solution.py:156
  102.9 2.4 %fusion.25 = f16[1024,256]{0,1:T(8,128)(2,1)S(1)} fusion(bf16[4096,256]{1,0:T(8,128)(2,1)S(1)} %constant_dynamic-update-slice_fusion.2, bf16[4096,2048]{1,0:T(8,128)(2,1)S(1)} %lagged.1), kind=kOutput, calls=%fused_computation.23 | convolution fusion | flops 2148007936 | bytes 11010048 | tf_op jit(solution)/shard_map/dot_general | solution.py:156
  105.3 1.3 collective-permute-start.25
  106.8 4.6 %collective-permute-start.12 = (f16[2048,128]{0,1:T(8,128)(2,1)S(1)}, f16[2048,128]{0,1:T(8,128)(2,1)S(1)}, u32[]{:S(2)}, u32[]{:S(2)}) collective-permute-start(f16[2048,128]{0,1:T(8,128)(2,1)S(1)} %get-tuple-element.22), channel_id=1, source_target_pairs={{0,8},{24,16},{1,9},{25,17},{2,10},{18,26},{3,11},{19,27},{12,4},{... | collective-permute-start | bytes 1572872 | tf_op jit(solution)/shard_map/ppermute | solution.py:188
  111.5 1.3 collective-permute-start.13
  112.8 1.6 collective-permute-start.18
  114.4 5.8 %fusion.8 = f16[2048,256]{0,1:T(8,128)(2,1)S(1)} fusion(bf16[4096,2048]{1,0:T(8,128)(2,1)S(1)} %lagged.1, bf16[4096,128]{1,0:T(8,128)(2,1)S(1)} %collective-permute-done.7, bf16[4096,128]{1,0:T(8,128)(2,1)} %copy-done.4), kind=kOutput, calls=%fused_computation.10 | convolution fusion | flops 4300210176 | bytes 19922944 | tf_op jit(solution)/shard_map/dot_general | solution.py:156
  120.3 1.5 collective-permute-start.15
  121.8 2.4 %fusion.34 = f16[1024,256]{0,1:T(8,128)(2,1)S(1)} fusion(bf16[4096,256]{1,0:T(8,128)(2,1)S(1)} %copy-done.2, bf16[4096,2048]{1,0:T(8,128)(2,1)S(1)} %lagged.1), kind=kOutput, calls=%fused_computation.26 | convolution fusion | flops 2148007936 | bytes 11010048 | tf_op jit(solution)/shard_map/dot_general | solution.py:156
  124.2 33.2 %collective-permute-done.18 = f16[2048,256]{0,1:T(8,128)(2,1)S(1)} collective-permute-done((f16[2048,256]{0,1:T(8,128)(2,1)S(1)}, f16[2048,256]{0,1:T(8,128)(2,1)S(1)}, u32[]{:S(2)}, u32[]{:S(2)}) %collective-permute-start.18) | collective-permute-done | bytes 1048608 | tf_op jit(solution)/shard_map/ppermute | solution.py:188
  157.4 4.4 %collective-permute-start.16 = (f16[2048,128]{0,1:T(8,128)(2,1)S(1)}, f16[2048,128]{0,1:T(8,128)(2,1)S(1)}, u32[]{:S(2)}, u32[]{:S(2)}) collective-permute-start(f16[2048,128]{0,1:T(8,128)(2,1)S(1)} %get-tuple-element.25), channel_id=1, source_target_pairs={{0,8},{24,16},{1,9},{25,17},{2,10},{18,26},{3,11},{19,27},{12,4},{... | collective-permute-start | bytes 1572872 | tf_op jit(solution)/shard_map/ppermute | solution.py:188
  162.3 1.3 collective-permute-start.9
  163.6 0.7 collective-permute-start.19
  164.8 3.9 %collective-permute-done.15 = f16[2048,128]{0,1:T(8,128)(2,1)S(1)} collective-permute-done((f16[2048,128]{0,1:T(8,128)(2,1)S(1)}, f16[2048,128]{0,1:T(8,128)(2,1)S(1)}, u32[]{:S(2)}, u32[]{:S(2)}) %collective-permute-start.15) | collective-permute-done | bytes 524320 | tf_op jit(solution)/shard_map/ppermute | solution.py:188
  168.7 0.7 collective-permute-start.14
  169.4 8.0 %collective-permute-done.16 = f16[2048,128]{0,1:T(8,128)(2,1)S(1)} collective-permute-done((f16[2048,128]{0,1:T(8,128)(2,1)S(1)}, f16[2048,128]{0,1:T(8,128)(2,1)S(1)}, u32[]{:S(2)}, u32[]{:S(2)}) %collective-permute-start.16) | collective-permute-done | bytes 524320 | tf_op jit(solution)/shard_map/ppermute | solution.py:188
  177.7 0.7 collective-permute-start.17
  178.4 1.0 add_convert_fusion.1
  179.5 1.3 collective-permute-start.27
  181.0 1.6 collective-permute-start.20
  182.6 0.7 fusion.44
  183.3 0.7 fusion.46
  184.2 0.7 fusion.38
  184.9 0.7 fusion.40
  185.5 29.8 %collective-permute-done.20 = f16[1024,256]{0,1:T(8,128)(2,1)S(1)} collective-permute-done((f16[1024,256]{0,1:T(8,128)(2,1)S(1)}, f16[1024,256]{0,1:T(8,128)(2,1)S(1)}, u32[]{:S(2)}, u32[]{:S(2)}) %collective-permute-start.20) | collective-permute-done | bytes 524320 | tf_op jit(solution)/shard_map/ppermute | solution.py:233
  216.5 1.3 copy-done
  217.8 1.5 convert_add_fusion
  219.6 1.2 multiply_dynamic-update-slice_fusion
  (68 shorter events, 8.4 us)
Async XLA Ops:
  2.8 8.9 %collective-permute-start.1 = (f32[3,256]{1,0:T(4,128)S(1)}, f32[3,256]{1,0:T(4,128)S(1)}, u32[]{:S(2)}, u32[]{:S(2)}) collective-permute-start(f32[3,256]{1,0:T(4,128)S(1)} %pad_maximum_fusion.3), channel_id=1, source_target_pairs={{0,8},{8,16},{16,24},{24,0},{1,9},{9,17},{17,25},{25,1},{2,10},{10... | collective-permute-start | bytes 9224 | tf_op jit(solution)/shard_map/ppermute | solution.py:117
  4.4 7.3 %collective-permute-start.2 = (f32[3,256]{1,0:T(4,128)S(1)}, f32[3,256]{1,0:T(4,128)S(1)}, u32[]{:S(2)}, u32[]{:S(2)}) collective-permute-start(f32[3,256]{1,0:T(4,128)S(1)} %pad_maximum_fusion.3), channel_id=1, source_target_pairs={{0,16},{8,24},{16,0},{24,8},{1,17},{9,25},{17,1},{25,9},{2,18},{10... | collective-permute-start | bytes 9224 | tf_op jit(solution)/shard_map/ppermute | solution.py:117
  7.0 4.7 %collective-permute-start.3 = (f32[3,256]{1,0:T(4,128)S(1)}, f32[3,256]{1,0:T(4,128)S(1)}, u32[]{:S(2)}, u32[]{:S(2)}) collective-permute-start(f32[3,256]{1,0:T(4,128)S(1)} %pad_maximum_fusion.3), channel_id=1, source_target_pairs={{0,24},{8,0},{16,8},{24,16},{1,25},{9,1},{17,9},{25,17},{2,26},{10... | collective-permute-start | bytes 9224 | tf_op jit(solution)/shard_map/ppermute | solution.py:117
  9.1 33.5 %collective-permute-start = (f32[16,256]{1,0:T(8,128)S(1)}, f32[16,256]{1,0:T(8,128)S(1)}, u32[]{:S(2)}, u32[]{:S(2)}) collective-permute-start(f32[16,256]{1,0:T(8,128)S(1)} %slice.230), channel_id=1, source_target_pairs={{0,8},{8,16},{16,24},{1,9},{9,17},{17,25},{2,10},{10,18},{18,26},{... | collective-permute-start | bytes 49160 | tf_op jit(solution)/shard_map/ppermute | solution.py:144
  13.7 2.7 %collective-permute-start.21 = (f32[1,256]{1,0:T(1,128)S(1)}, f32[1,256]{1,0:T(1,128)S(1)}, u32[]{:S(2)}, u32[]{:S(2)}) collective-permute-start(f32[1,256]{1,0:T(1,128)S(1)} %get-tuple-element.26), channel_id=1, source_target_pairs={{0,1},{1,0},{2,3},{3,2},{4,5},{5,4},{6,7},{7,6},{8,9},{9,8},{10,11... | collective-permute-start | bytes 3080 | tf_op jit(solution)/shard_map/ppermute | solution.py:149
  15.8 32.8 %collective-permute-start.7 = (bf16[4096,128]{1,0:T(8,128)(2,1)S(1)}, bf16[4096,128]{1,0:T(8,128)(2,1)S(1)}, u32[]{:S(2)}, u32[]{:S(2)}) collective-permute-start(bf16[4096,128]{1,0:T(8,128)(2,1)S(1)} %multiply_convert_fusion), channel_id=1, source_target_pairs={{0,4},{1,5},{2,6},{3,7},{4,0},{5,1},{6,2},{7,3},{8,12},{9,13},{10,... | collective-permute-start | bytes 3145736 | tf_op jit(solution)/shard_map/ppermute | solution.py:142
  16.3 4.6 %collective-permute-start.22 = (f32[2,256]{1,0:T(2,128)S(1)}, f32[2,256]{1,0:T(2,128)S(1)}, u32[]{:S(2)}, u32[]{:S(2)}) collective-permute-start(f32[2,256]{1,0:T(2,128)S(1)} %pad_maximum_fusion.4), channel_id=1, source_target_pairs={{0,6},{1,7},{2,4},{3,5},{4,2},{5,3},{6,0},{7,1},{8,14},{9,15},{10,... | collective-permute-start | bytes 6152 | tf_op jit(solution)/shard_map/ppermute | solution.py:153
  17.9 23.6 %collective-permute-start.23 = (f32[2,256]{1,0:T(2,128)S(1)}, f32[2,256]{1,0:T(2,128)S(1)}, u32[]{:S(2)}, u32[]{:S(2)}) collective-permute-start(f32[2,256]{1,0:T(2,128)S(1)} %pad_maximum_fusion.4), channel_id=1, source_target_pairs={{0,4},{1,5},{2,6},{3,7},{4,0},{5,1},{6,2},{7,3},{8,12},{9,13},{10,... | collective-permute-start | bytes 6152 | tf_op jit(solution)/shard_map/ppermute | solution.py:153
  18.4 23.6 %collective-permute-start.24 = (f32[2,256]{1,0:T(2,128)S(1)}, f32[2,256]{1,0:T(2,128)S(1)}, u32[]{:S(2)}, u32[]{:S(2)}) collective-permute-start(f32[2,256]{1,0:T(2,128)S(1)} %pad_maximum_fusion.4), channel_id=1, source_target_pairs={{0,2},{1,3},{2,0},{3,1},{4,6},{5,7},{6,4},{7,5},{8,10},{9,11},{10,... | collective-permute-start | bytes 6152 | tf_op jit(solution)/shard_map/ppermute | solution.py:153
  21.0 25.6 %collective-permute-start.5 = (bf16[4096,128]{1,0:T(8,128)(2,1)S(1)}, bf16[4096,128]{1,0:T(8,128)(2,1)S(1)}, u32[]{:S(2)}, u32[]{:S(2)}) collective-permute-start(bf16[4096,128]{1,0:T(8,128)(2,1)S(1)} %multiply_convert_fusion.1), channel_id=1, source_target_pairs={{0,2},{1,3},{2,0},{3,1},{4,6},{5,7},{6,4},{7,5},{8,10},{9,11},{10,... | collective-permute-start | bytes 3145736 | tf_op jit(solution)/shard_map/ppermute | solution.py:142
  41.5 27.6 %collective-permute-start.10 = (bf16[4096,128]{1,0:T(8,128)(2,1)S(1)}, bf16[4096,128]{1,0:T(8,128)(2,1)S(1)}, u32[]{:S(2)}, u32[]{:S(2)}) collective-permute-start(bf16[4096,128]{1,0:T(8,128)(2,1)S(1)} %multiply_convert_fusion), channel_id=1, source_target_pairs={{0,2},{1,3},{2,0},{3,1},{4,6},{5,7},{6,4},{7,5},{8,10},{9,11},{10,... | collective-permute-start | bytes 3145736 | tf_op jit(solution)/shard_map/ppermute | solution.py:142
  42.0 27.2 %collective-permute-start.11 = (bf16[4096,128]{1,0:T(8,128)(2,1)S(1)}, bf16[4096,128]{1,0:T(8,128)(2,1)S(1)}, u32[]{:S(2)}, u32[]{:S(2)}) collective-permute-start(bf16[4096,128]{1,0:T(8,128)(2,1)S(1)} %multiply_convert_fusion.1), channel_id=1, source_target_pairs={{0,4},{1,5},{2,6},{3,7},{4,0},{5,1},{6,2},{7,3},{8,12},{9,13},{10,... | collective-permute-start | bytes 3145736 | tf_op jit(solution)/shard_map/ppermute | solution.py:142
  42.7 47.6 %collective-permute-start.4 = (bf16[4112,256]{1,0:T(8,128)(2,1)S(1)}, bf16[4112,256]{1,0:T(8,128)(2,1)S(1)}, u32[]{:S(2)}, u32[]{:S(2)}) collective-permute-start(bf16[4112,256]{1,0:T(8,128)(2,1)S(1)} %pad_maximum_fusion.own_ref.own_next_ref), channel_id=1, source_target_pairs={{0,1},{1,0},{2,3},{3,2},{4,5},{5,4},{6,7},{7,6},{8,9},{9,8},{10,11... | collective-permute-start | bytes 6316040 | tf_op jit(solution)/shard_map/ppermute | solution.py:147
  46.6 43.8 %copy-start.4 = (bf16[4096,128]{1,0:T(8,128)(2,1)}, bf16[4096,128]{1,0:T(8,128)(2,1)S(1)}, u32[]{:S(2)}) copy-start(bf16[4096,128]{1,0:T(8,128)(2,1)S(1)} %collective-permute-done.5) | copy-start | bytes 3145732
  46.6 42.3 %collective-permute-start.6 = (bf16[4096,128]{1,0:T(8,128)(2,1)S(1)}, bf16[4096,128]{1,0:T(8,128)(2,1)S(1)}, u32[]{:S(2)}, u32[]{:S(2)}) collective-permute-start(bf16[4096,128]{1,0:T(8,128)(2,1)S(1)} %collective-permute-done.5), channel_id=1, source_target_pairs={{0,4},{1,5},{2,6},{3,7},{4,0},{5,1},{6,2},{7,3},{8,12},{9,13},{10,... | collective-permute-start | bytes 3145736 | tf_op jit(solution)/shard_map/ppermute | solution.py:200
  48.6 41.5 %collective-permute-start.8 = (bf16[4096,128]{1,0:T(8,128)(2,1)S(1)}, bf16[4096,128]{1,0:T(8,128)(2,1)S(1)}, u32[]{:S(2)}, u32[]{:S(2)}) collective-permute-start(bf16[4096,128]{1,0:T(8,128)(2,1)S(1)} %collective-permute-done.7), channel_id=1, source_target_pairs={{0,2},{1,3},{2,0},{3,1},{4,6},{5,7},{6,4},{7,5},{8,10},{9,11},{10,... | collective-permute-start | bytes 3145736 | tf_op jit(solution)/shard_map/ppermute | solution.py:200
  90.3 12.6 %copy-start.1 = (bf16[4096,256]{1,0:T(8,128)(2,1)}, bf16[4096,256]{1,0:T(8,128)(2,1)S(1)}, u32[]{:S(2)}) copy-start(bf16[4096,256]{1,0:T(8,128)(2,1)S(1)} %constant_dynamic-update-slice_fusion.2) | copy-start | bytes 6291460
  105.3 73.1 %collective-permute-start.25 = (f16[1024,256]{0,1:T(8,128)(2,1)S(1)}, f16[1024,256]{0,1:T(8,128)(2,1)S(1)}, u32[]{:S(2)}, u32[]{:S(2)}) collective-permute-start(f16[1024,256]{0,1:T(8,128)(2,1)S(1)} %fusion.25), channel_id=1, source_target_pairs={{0,8},{16,24},{1,9},{17,25},{2,10},{26,18},{3,11},{27,19},{4,12},{... | collective-permute-start | bytes 1572872 | tf_op jit(solution)/shard_map/ppermute | solution.py:188
  106.8 55.4 %collective-permute-start.12 = (f16[2048,128]{0,1:T(8,128)(2,1)S(1)}, f16[2048,128]{0,1:T(8,128)(2,1)S(1)}, u32[]{:S(2)}, u32[]{:S(2)}) collective-permute-start(f16[2048,128]{0,1:T(8,128)(2,1)S(1)} %get-tuple-element.22), channel_id=1, source_target_pairs={{0,8},{24,16},{1,9},{25,17},{2,10},{18,26},{3,11},{19,27},{12,4},{... | collective-permute-start | bytes 1572872 | tf_op jit(solution)/shard_map/ppermute | solution.py:188
  111.5 52.1 %collective-permute-start.13 = (f16[2048,128]{0,1:T(8,128)(2,1)S(1)}, f16[2048,128]{0,1:T(8,128)(2,1)S(1)}, u32[]{:S(2)}, u32[]{:S(2)}) collective-permute-start(f16[2048,128]{0,1:T(8,128)(2,1)S(1)} %get-tuple-element.23), channel_id=1, source_target_pairs={{0,8},{24,16},{1,9},{25,17},{10,2},{26,18},{11,3},{27,19},{4,12},{... | collective-permute-start | bytes 1572872 | tf_op jit(solution)/shard_map/ppermute | solution.py:188
  112.8 44.6 %collective-permute-start.18 = (f16[2048,256]{0,1:T(8,128)(2,1)S(1)}, f16[2048,256]{0,1:T(8,128)(2,1)S(1)}, u32[]{:S(2)}, u32[]{:S(2)}) collective-permute-start(f16[2048,256]{0,1:T(8,128)(2,1)S(1)} %fusion.9), channel_id=1, source_target_pairs={{8,0},{24,16},{9,1},{25,17},{2,10},{26,18},{3,11},{27,19},{4,12},{... | collective-permute-start | bytes 3145736 | tf_op jit(solution)/shard_map/ppermute | solution.py:188
  120.1 1.7 copy-start.2
  120.3 48.3 %collective-permute-start.15 = (f16[2048,128]{0,1:T(8,128)(2,1)S(1)}, f16[2048,128]{0,1:T(8,128)(2,1)S(1)}, u32[]{:S(2)}, u32[]{:S(2)}) collective-permute-start(f16[2048,128]{0,1:T(8,128)(2,1)S(1)} %get-tuple-element.24), channel_id=1, source_target_pairs={{0,8},{24,16},{1,9},{25,17},{10,2},{26,18},{11,3},{27,19},{4,12},{... | collective-permute-start | bytes 1572872 | tf_op jit(solution)/shard_map/ppermute | solution.py:188
  157.4 19.9 %collective-permute-start.16 = (f16[2048,128]{0,1:T(8,128)(2,1)S(1)}, f16[2048,128]{0,1:T(8,128)(2,1)S(1)}, u32[]{:S(2)}, u32[]{:S(2)}) collective-permute-start(f16[2048,128]{0,1:T(8,128)(2,1)S(1)} %get-tuple-element.25), channel_id=1, source_target_pairs={{0,8},{24,16},{1,9},{25,17},{2,10},{18,26},{3,11},{19,27},{12,4},{... | collective-permute-start | bytes 1572872 | tf_op jit(solution)/shard_map/ppermute | solution.py:188
  162.3 18.5 %collective-permute-start.9 = (f16[1024,256]{0,1:T(8,128)(2,1)S(1)}, f16[1024,256]{0,1:T(8,128)(2,1)S(1)}, u32[]{:S(2)}, u32[]{:S(2)}) collective-permute-start(f16[1024,256]{0,1:T(8,128)(2,1)S(1)} %fusion.34), channel_id=1, source_target_pairs={{0,8},{16,24},{1,9},{17,25},{2,10},{26,18},{3,11},{27,19},{4,12},{... | collective-permute-start | bytes 1572872 | tf_op jit(solution)/shard_map/ppermute | solution.py:188
  163.6 19.0 %collective-permute-start.19 = (f16[2048,256]{0,1:T(8,128)(2,1)S(1)}, f16[2048,256]{0,1:T(8,128)(2,1)S(1)}, u32[]{:S(2)}, u32[]{:S(2)}) collective-permute-start(f16[2048,256]{0,1:T(8,128)(2,1)S(1)} %add_convert_fusion), channel_id=1, source_target_pairs={{16,0},{17,1},{18,10},{19,11},{12,20},{13,21},{14,30},{15,31}} | collective-permute-start | bytes 3145736 | tf_op jit(solution)/shard_map/ppermute | solution.py:193
  168.7 13.9 %collective-permute-start.14 = (f16[2048,128]{0,1:T(8,128)(2,1)S(1)}, f16[2048,128]{0,1:T(8,128)(2,1)S(1)}, u32[]{:S(2)}, u32[]{:S(2)}) collective-permute-start(f16[2048,128]{0,1:T(8,128)(2,1)S(1)} %select_convert_fusion.1), channel_id=1, source_target_pairs={{16,8},{17,9},{18,2},{19,3},{12,28},{13,29},{14,22},{15,23},{8,16}... | collective-permute-start | bytes 1572872 | tf_op jit(solution)/shard_map/ppermute | solution.py:224
  177.7 4.8 %collective-permute-start.17 = (f16[2048,128]{0,1:T(8,128)(2,1)S(1)}, f16[2048,128]{0,1:T(8,128)(2,1)S(1)}, u32[]{:S(2)}, u32[]{:S(2)}) collective-permute-start(f16[2048,128]{0,1:T(8,128)(2,1)S(1)} %select_convert_fusion), channel_id=1, source_target_pairs={{16,8},{17,9},{18,2},{19,3},{12,28},{13,29},{14,22},{15,23},{8,16}... | collective-permute-start | bytes 1572872 | tf_op jit(solution)/shard_map/ppermute | solution.py:224
  179.5 37.0 %collective-permute-start.27 = (f16[1024,256]{0,1:T(8,128)(2,1)}, f16[1024,256]{0,1:T(8,128)(2,1)}, u32[]{:S(2)}, u32[]{:S(2)}) collective-permute-start(f16[1024,256]{0,1:T(8,128)(2,1)} %add_convert_fusion.1), channel_id=1, source_target_pairs={{8,25},{9,24},{10,19},{11,18},{20,13},{21,12},{22,7},{23,6}} | collective-permute-start | bytes 1572872 | tf_op jit(solution)/shard_map/ppermute | solution.py:233
  181.0 34.4 %collective-permute-start.20 = (f16[1024,256]{0,1:T(8,128)(2,1)S(1)}, f16[1024,256]{0,1:T(8,128)(2,1)S(1)}, u32[]{:S(2)}, u32[]{:S(2)}) collective-permute-start(f16[1024,256]{0,1:T(8,128)(2,1)S(1)} %add_convert_fusion.2), channel_id=1, source_target_pairs={{8,24},{9,25},{10,18},{11,19},{20,12},{21,13},{22,6},{23,7}} | collective-permute-start | bytes 1572872 | tf_op jit(solution)/shard_map/ppermute | solution.py:233
  184.1 33.7 %collective-permute-start.26 = (f32[1024,256]{0,1:T(8,128)S(1)}, f32[1024,256]{0,1:T(8,128)}, u32[]{:S(2)}, u32[]{:S(2)}) collective-permute-start(f32[1024,256]{0,1:T(8,128)S(1)} %pad_maximum_fusion.1), channel_id=1, source_target_pairs={{0,1},{1,0},{2,3},{3,2},{4,5},{5,4},{6,7},{7,6},{8,9},{9,8},{10,11... | collective-permute-start | bytes 3145736 | tf_op jit(solution)/shard_map/ppermute | solution.py:251
  215.6 0.7 copy-start.3
  216.4 1.3 copy-start

commit v2 on v1

--- a/solution.py
+++ b/solution.py
@@ -49,49 +49,83 @@
     return levels
 
 
-def lagged_kernel(own_ref, own_next_ref, other_ref, other_next_ref, out_ref, wide_ref, exact_ref):
-    rows, cols = own_ref.shape
-    for i, (ref, after) in enumerate(((own_ref, own_next_ref), (other_ref, other_next_ref))):
-        exact_ref[:rows] = ref[...]
-        exact_ref[rows:] = after[...]
-        wide_ref[:rows] = ref[...].astype(jnp.float32)
-        wide_ref[rows:] = after[...].astype(jnp.float32)
+def lagged_kernel(*refs):
+    out_ref, wide_ref, exact_ref = refs[-3:]
+    rows, cols = wide_ref.shape[0] - HALO, wide_ref.shape[1]
+    half = cols // 2
+    step = pl.program_id(0)
+    here = pl.ds(pl.multiple_of(step * rows, rows), rows)
+    for i in (0, 1):
+        first_ref, *parts = refs[5 * i : 5 * i + 5]
+        for h in (0, 1):
+            main_ref, prior_ref = parts[2 * h : 2 * h + 2]
+            columns = slice(h * half, (h + 1) * half)
+            prior = jnp.where(step == 0, first_ref[:, columns], prior_ref[...])
+            exact_ref[:HALO, columns] = prior
+            exact_ref[HALO:, columns] = main_ref[...]
+            wide_ref[:HALO, columns] = prior.astype(jnp.float32)
+            wide_ref[HALO:, columns] = main_ref[...].astype(jnp.float32)
         for k, lag in enumerate(LAGS):
             start = HALO - lag
             source = exact_ref if start % 16 == 0 else wide_ref
             at = (len(LAGS) * i + k) * cols
-            out_ref[:, at : at + cols] = source[start : start + rows].astype(out_ref.dtype)
+            out_ref[here, at : at + cols] = source[start : start + rows].astype(out_ref.dtype)
 
 
 def lagged_columns(own, other):
-    rows, cols = own.shape[0] - HALO, own.shape[1]
+    rows, half = own[1].shape
+    cols = 2 * half
     step = math.gcd(rows, 512)
-    main = pl.BlockSpec((step, cols), lambda i: (i, 0))
-    after = pl.BlockSpec((HALO, cols), lambda i: ((i + 1) * (step // HALO), 0))
     wide = 2 * len(LAGS) * cols
-
-    def body(own_ref, own_next_ref, other_ref, other_next_ref, out_ref, wide_ref, exact_ref):
-        rows_here = pl.ds(pl.multiple_of(pl.program_id(0) * step, step), step)
-        lagged_kernel(
-            own_ref, own_next_ref, other_ref, other_next_ref, out_ref.at[rows_here], wide_ref, exact_ref
-        )
-
+    first = pl.BlockSpec((HALO, cols), lambda i: (0, 0))
+    main = pl.BlockSpec((step, half), lambda i: (i, 0))
+    prior = pl.BlockSpec((HALO, half), lambda i: (jnp.maximum(i * (step // HALO) - 1, 0), 0))
+    operands = [v for before, a, b in (own, other) for v in (before, a, a, b, b)]
     return pl.pallas_call(
-        body,
-        out_shape=pltpu.VMEM((rows, wide), own.dtype),
+        lagged_kernel,
+        out_shape=pltpu.VMEM((rows, wide), own[1].dtype),
         grid=(rows // step,),
-        in_specs=[main, after, main, after],
+        in_specs=[first, main, prior, main, prior] * 2,
         out_specs=pl.BlockSpec(memory_space=pltpu.VMEM),
         scratch_shapes=[
             pltpu.VMEM((step + HALO, cols), jnp.float32),
-            pltpu.VMEM((step + HALO, cols), own.dtype),
+            pltpu.VMEM((step + HALO, cols), own[1].dtype),
         ],
         cost_estimate=pl.CostEstimate(
             flops=rows * wide, bytes_accessed=2 * rows * (wide + 2 * cols), transcendentals=0
         ),
         compiler_params=pltpu.CompilerParams(vmem_limit_bytes=16 * 1024 * 1024),
         name="lagged",
-    )(own, own, other, other)
+    )(*operands)
+
+
+def join_kernel(left_ref, right_ref, out_ref, sems):
+    cols = left_ref.shape[1]
+    copies = [
+        pltpu.make_async_copy(ref, out_ref.at[:, i * cols : (i + 1) * cols], sems.at[i])
+        for i, ref in enumerate((left_ref, right_ref))
+    ]
+    for copy in copies:
+        copy.start()
+    for copy in copies:
+        copy.wait()
+
+
+def joined(left, right):
+    rows, cols = left.shape
+    anywhere = pl.BlockSpec(memory_space=pl.ANY)
+    if cols % 128:
+        return jnp.concatenate([left, right], 1)
+    return pl.pallas_call(
+        join_kernel,
+        out_shape=pltpu.VMEM((rows, 2 * cols), left.dtype),
+        in_specs=[anywhere, anywhere],
+        out_specs=pl.BlockSpec(memory_space=pltpu.VMEM),
+        scratch_shapes=[pltpu.SemaphoreType.DMA((2,))],
+        cost_estimate=pl.CostEstimate(flops=0, bytes_accessed=8 * rows * cols, transcendentals=0),
+        compiler_params=pltpu.CompilerParams(vmem_limit_bytes=1024 * 1024),
+        name="join",
+    )(left, right)
 
 
 def make(mesh):
@@ -141,10 +175,13 @@
                 if len(bits(m)) == 1:
                     got[m, h] = lax.ppermute(got[0, h], "feat", hop(2 * m))
 
-        before = lax.ppermute(trajectory[rows - HALO :], "tm", [(i, i + 1) for i in range(nz - 1)])
+        swapped = [lax.ppermute(got[0, h], "feat", hop(1)) for h in (0, 1)]
+        tail, got[0, 1] = lax.optimization_barrier((trajectory, got[0, 1]))
+        before = lax.ppermute(tail[rows - HALO :], "tm", [(i, i + 1) for i in range(nz - 1)])
         first = jnp.where(z == 0, jnp.bfloat16(0), centre(before))
-        own = jnp.concatenate([first, jnp.concatenate([got[0, 0], got[0, 1]], 1)])
-        lagged = lagged_columns(own, lax.ppermute(own, "feat", hop(1)))
+        lagged = lagged_columns(
+            (first, got[0, 0], got[0, 1]), (lax.ppermute(first, "feat", hop(1)), *swapped)
+        )
 
         turned = lax.ppermute(grow[None], "feat", hop(1))[0]
         pair = jnp.stack([jnp.where(core == 0, grow, turned), jnp.where(core == 0, turned, grow)])
@@ -152,10 +189,10 @@
         for m in range(1, chips):
             across = jnp.where(mine == m, lax.ppermute(pair, "feat", hop(2 * m)), across)
 
-        def product(blocks, low=0, high=2 * tall):
+        def product(block, low=0, high=2 * tall):
             value = lax.dot_general(
+                block,
                 lagged[:, low:high],
-                jnp.concatenate(blocks, 1) if len(blocks) > 1 else blocks[0],
                 (((0,), (0,)), ((), ())),
                 preferred_element_type=jnp.float32,
             )
@@ -188,10 +225,10 @@
                 terms.append(lax.ppermute(sent, both, rise(mask, level)))
             return terms
 
-        part = product([own[HALO:]])
+        part = product(joined(got[0, 0], got[0, 1]))
         terms = climbed(part, 0, top)
         terms.append(lax.ppermute(add(terms).astype(jnp.float16), both, rise(0, top)))
-        kept = [[(0, [v[:, h * half : (h + 1) * half] for v in terms])] for h in (0, 1)]
+        kept = [[(0, [v[h * half : (h + 1) * half] for v in terms])] for h in (0, 1)]
 
         for slot in slots:
             for m, h in slot:
@@ -200,62 +237,61 @@
                     got[m, h] = lax.ppermute(got[m ^ axis, h], "feat", hop(2 * axis))
 
         late = [[], []]
-        for s, slot in enumerate(slots):
+        for slot in slots:
             (a, ha), (b, hb) = slot
-            blocks = [got[u] for u in slot]
+            block = joined(*[got[u] for u in slot])
             if a != b:
-                if s == 0:
-                    part = product(blocks)
-                else:
-                    part = jnp.concatenate(
-                        [product(blocks, i * tall, (i + 1) * tall) for i in (0, 1)]
-                    )
-                sides = [
-                    climbed(part[:, i * half : (i + 1) * half], m, top)
-                    for i, (m, _) in enumerate(slot)
-                ]
-                pairs = rise(a, top) + rise(b, top)
-                assert all(len({p[i] for p in pairs}) == len(pairs) for i in (0, 1))
-                sender = sum(
-                    jnp.where(lax.bitwise_xor(chip, a) == q, tree_levels(q, nz)[top][0][0], 0)
-                    for q in range(nz)
-                )
-                sent = jnp.where(z == sender, *map(add, sides)).astype(jnp.float16)
-                back = lax.ppermute(sent, both, pairs)
-                kept[ha].append((a, sides[0] + [back]))
-                kept[hb].append((b, sides[1] + [back]))
+                part = product(block)
+                sides = [part[:half], part[half:]]
+                terms = [jnp.where(mine == a, *sides)]
+                for k in range(1, nz):
+                    pairs = [
+                        (y * nf + i, (y ^ k) * nf + i)
+                        for i in range(nf)
+                        for y in range(nz)
+                        if i // 2 ^ y ^ k in (a, b)
+                    ]
+                    sent = jnp.where(lax.bitwise_xor(mine, k) == a, *sides)
+                    terms.append(lax.ppermute(sent, both, pairs))
+                kept[ha].append((a, terms))
+                kept[hb].append((b, terms))
                 continue
             sums = []
             for i in (0, 1):
-                part = product(blocks, i * tall, (i + 1) * tall)
+                part = product(block, i * tall, (i + 1) * tall)
                 terms = climbed(part, a, top)
                 sent = add(terms).astype(jnp.float16)
                 late[i].append(lax.ppermute(sent, both, rise(a, top, i)))
                 sums.append(terms)
-            kept[ha].append((a, [[v[:, :half] for v in terms] for terms in sums]))
-            kept[hb].append((b, [[v[:, half:] for v in terms] for terms in sums]))
-
-        sides = []
-        for i in (0, 1):
-            columns = []
-            for h in (0, 1):
-                total = none
-                for m, terms in kept[h]:
-                    if isinstance(terms[0], list):
-                        terms = terms[i]
-                    else:
-                        terms = [v[i * tall : (i + 1) * tall] for v in terms]
-                    total = jnp.where(mine == m, add(terms), total)
-                columns.append(total)
-            sides.append(jnp.concatenate(columns, 1))
+            kept[ha].append((a, [[v[:half] for v in terms] for terms in sums]))
+            kept[hb].append((b, [[v[half:] for v in terms] for terms in sums]))
+
+        def owned(m):
+            terms = [dict(kept[h])[m] for h in (0, 1)]
+
+            def branch(both_terms):
+                sides = []
+                for i in (0, 1):
+                    columns = []
+                    for values in both_terms:
+                        if isinstance(values[0], list):
+                            values = values[i]
+                        else:
+                            values = [v[:, i * tall : (i + 1) * tall] for v in values]
+                        columns.append(add(values))
+                    sides.append(jnp.concatenate(columns))
+                return sides
+
+            return lambda: branch(terms)
+
+        sides = lax.switch(mine, [owned(m) for m in range(chips)])
         near, theirs = sides[0], lax.ppermute(sides[1], "feat", hop(1))
-
         scales = 1 / (jnp.sqrt(jnp.float32(frames) - jnp.array(LAGS, jnp.float32)) * room)
         out = jnp.zeros((len(LAGS), cols, 2 * cols), jnp.float32)
         for value, added, owner in ((near, late[0], core), (theirs, late[1], 1 - core)):
             for more in added:
                 value = value + wide(more)
-            value = value.reshape(len(LAGS), cols, cols) * scales[:, None, None]
+            value = value.T.reshape(len(LAGS), cols, cols) * scales[:, None, None]
             value = value * grow[None, :, None] * jnp.where(owner == 0, across[0], across[1])
             out = lax.dynamic_update_slice(out, value, (0, 0, owner * cols))
         return out

time: 221 us -> 204 us (0.923)
  the two profiles are of different devices: /device:TPU:6 before, /device:TPU:13 now
where the time goes in v2:
time: 204 us; the launch traced here: 203 us
  waiting for transfers between devices  94.4 us (46%)
  starting transfers between devices  59.7 us (29%)
  matrix products  19.1 us (9%)
  other arithmetic  18.1 us (9%)
  Pallas kernels  9.02 us (4%)
  local copies, waits for them, and re-layouts  2.54 us (1%)
    ppermute x6, waiting for transfers between devices, shards(): terms.append(lax.ppermute(sent, both, pairs))  26.7 us
    ppermute x3, waiting for transfers between devices, climbed(): terms.append(lax.ppermute(sent, both, rise(mask, level)))  19.7 us
    dot_general x5, matrix products, product(): lax.dot_general(block, lagged[:, low:high], (((0,), (0,)), ((), ())), pre...  19.1 us
    ppermute x1, starting transfers between devices, shards(): near, theirs = (sides[0], lax.ppermute(sides[1], 'feat', hop(1)))  17.2 us
    ppermute x4, waiting for transfers between devices, shards(): got[m, h] = lax.ppermute(got[0, h], 'feat', hop(2 * m))  16.7 us
    ppermute x6, starting transfers between devices, shards(): terms.append(lax.ppermute(sent, both, pairs))  15 us
    ppermute x2, waiting for transfers between devices, shards(): got[m, h] = lax.ppermute(got[m ^ axis, h], 'feat', hop(2 * axis))  13.6 us
    ppermute x2, waiting for transfers between devices, shards(): late[i].append(lax.ppermute(sent, both, rise(a, top, i)))  12.4 us
  transfers between devices with their start and end apart: 30, of which 12 were waited for; matrix products, arithmetic and copies ran while one was open for 16% of the time, Pallas kernels for 4%

profile of v2, /device:TPU:13, one launch (start us, length us, event | category | flops | bytes accessed | tf_op | source)
XLA Modules:
  0.0 203.2 jit_solution(8064879523214712424)
XLA Ops:
  0.0 2.9 %fusion.20 = (f32[256]{0:T(256)S(1)}, f32[256]{0:T(256)S(1)}, f32[256]{0:T(256)S(1)}) fusion(f32[4096,256]{1,0:T(8,128)} %param.6), kind=kLoop, calls=%fused_computation.69 | loop fusion | flops 3144960 | bytes 4197376 | tf_op jit(solution)/shard_map/reduce_sum | solution.py:149
  2.9 1.3 collective-permute-start
  4.3 1.1 collective-permute-start.1
  5.4 1.4 collective-permute-start.2
  8.4 1.3 collective-permute-start.14
  9.9 2.8 %collective-permute-start.6 = (bf16[4096,128]{1,0:T(8,128)(2,1)S(1)}, bf16[4096,128]{1,0:T(8,128)(2,1)S(1)}, u32[]{:S(2)}, u32[]{:S(2)}) collective-permute-start(bf16[4096,128]{1,0:T(8,128)(2,1)S(1)} %multiply_convert_fusion.right_ref.refs_3_.refs_4_), channel_id=1, source_target_pairs={{0,1},{1,0},{2,3},{3,2},{4,5},{5,4},{6,7},{7,6},{8,9},{9,8},{10,11... | collective-permute-start | bytes 3145736 | tf_op jit(solution)/shard_map/ppermute | solution.py:178
  14.4 2.3 %collective-permute-done.24 = f32[1,256]{1,0:T(1,128)S(1)} collective-permute-done((f32[1,256]{1,0:T(1,128)S(1)}, f32[1,256]{1,0:T(1,128)S(1)}, u32[]{:S(2)}, u32[]{:S(2)}) %collective-permute-start.24) | collective-permute-done | bytes 1056 | tf_op jit(solution)/shard_map/ppermute | solution.py:186
  16.7 3.0 %collective-permute-start.3 = (f32[16,256]{1,0:T(8,128)S(1)}, f32[16,256]{1,0:T(8,128)S(1)}, u32[]{:S(2)}, u32[]{:S(2)}) collective-permute-start(f32[16,256]{1,0:T(8,128)S(1)} %slice.277), channel_id=1, source_target_pairs={{0,8},{8,16},{16,24},{1,9},{9,17},{17,25},{2,10},{10,18},{18,26},{... | collective-permute-start | bytes 49160 | tf_op jit(solution)/shard_map/ppermute | solution.py:180
  19.7 1.8 collective-permute-done.3
  21.5 1.1 collective-permute-start.4
  22.7 8.4 %collective-permute-done.14.left_ref = bf16[4096,128]{1,0:T(8,128)(2,1)} collective-permute-done((bf16[4096,128]{1,0:T(8,128)(2,1)S(1)}, bf16[4096,128]{1,0:T(8,128)(2,1)}, u32[]{:S(2)}, u32[]{:S(2)}) %collective-permute-start.14) | collective-permute-done | bytes 1048608 | tf_op jit(solution)/shard_map/ppermute | solution.py:176
  32.5 1.6 join.6
  34.1 1.3 collective-permute-start.25
  35.4 0.9 collective-permute-start.26
  36.3 6.3 %lagged.1 = bf16[4096,2048]{1,0:T(8,128)(2,1)S(1)} custom-call(bf16[16,256]{1,0:T(8,128)(2,1)S(1)} %fusion.19.refs_0_, bf16[4096,128]{1,0:T(8,128)(2,1)S(1)} %multiply_convert_fusion.1.left_ref.refs_1_.refs_2_, bf16[4096,128]{1,0:T(8,128)(2,1)S(1)} %multiply_convert_fusion.1.left_ref.refs_1_.refs_2_, ...), custom_call_target="tpu_custom_call" | custom-call | flops 8388608 | bytes 20971520 | tf_op jit(solution)/shard_map/lagged/pallas_call | solution.py:84
  42.6 4.5 %fusion.6 = f16[256,2048]{1,0:T(8,128)(2,1)S(1)} fusion(bf16[4096,256]{1,0:T(8,128)(2,1)S(1)} %join.6, bf16[4096,2048]{1,0:T(8,128)(2,1)S(1)} %lagged.1), kind=kOutput, calls=%fused_computation.33 | convolution fusion | flops 4296015872 | bytes 19922944 | tf_op jit(solution)/shard_map/dot_general | solution.py:193
  47.1 7.8 %collective-permute-done.10.right_ref = bf16[4096,128]{1,0:T(8,128)(2,1)S(1)} collective-permute-done((bf16[4096,128]{1,0:T(8,128)(2,1)S(1)}, bf16[4096,128]{1,0:T(8,128)(2,1)S(1)}, u32[]{:S(2)}, u32[]{:S(2)}) %collective-permute-start.10) | collective-permute-done | bytes 1048608 | tf_op jit(solution)/shard_map/ppermute | solution.py:176
  55.3 4.5 %fusion.5 = f16[256,2048]{1,0:T(8,128)(2,1)S(1)} fusion(bf16[4096,256]{1,0:T(8,128)(2,1)S(1)} %join.5, bf16[4096,2048]{1,0:T(8,128)(2,1)S(1)} %lagged.1), kind=kOutput, calls=%fused_computation.32 | convolution fusion | flops 4296015872 | bytes 19922944 | tf_op jit(solution)/shard_map/dot_general | solution.py:193
  60.2 4.5 %fusion.4 = f16[256,2048]{1,0:T(8,128)(2,1)S(1)} fusion(bf16[4096,256]{1,0:T(8,128)(2,1)S(1)} %join.4, bf16[4096,2048]{1,0:T(8,128)(2,1)S(1)} %lagged.1), kind=kOutput, calls=%fused_computation.31 | convolution fusion | flops 4296015872 | bytes 19922944 | tf_op jit(solution)/shard_map/dot_general | solution.py:193
  64.7 1.5 collective-permute-start.7
  66.6 1.5 broadcast_select_fusion.1
  68.1 13.6 %collective-permute-done.20.right_ref = bf16[4096,128]{1,0:T(8,128)(2,1)S(1)} collective-permute-done((bf16[4096,128]{1,0:T(8,128)(2,1)S(1)}, bf16[4096,128]{1,0:T(8,128)(2,1)S(1)}, u32[]{:S(2)}, u32[]{:S(2)}) %collective-permute-start.20) | collective-permute-done | bytes 1048608 | tf_op jit(solution)/shard_map/ppermute | solution.py:237
  81.7 3.6 %collective-permute-start.16 = (f16[128,2048]{1,0:T(8,128)(2,1)S(1)}, f16[128,2048]{1,0:T(8,128)(2,1)S(1)}, u32[]{:S(2)}, u32[]{:S(2)}) collective-permute-start(f16[128,2048]{1,0:T(8,128)(2,1)S(1)} %get-tuple-element.147), channel_id=1, source_target_pairs={{0,8},{24,16},{1,9},{25,17},{10,2},{18,26},{11,3},{19,27},{12,4},{... | collective-permute-start | bytes 1572872 | tf_op jit(solution)/shard_map/ppermute | solution.py:255
  85.7 2.4 %fusion.16 = f16[256,1024]{1,0:T(8,128)(2,1)S(1)} fusion(bf16[4096,256]{1,0:T(8,128)(2,1)S(1)} %join.7, bf16[4096,2048]{1,0:T(8,128)(2,1)S(1)} %lagged.1), kind=kOutput, calls=%fused_computation.40 | convolution fusion | flops 2148007936 | bytes 11010048 | tf_op jit(solution)/shard_map/dot_general | solution.py:193
  88.2 2.7 %collective-permute-start.17 = (f16[128,2048]{1,0:T(8,128)(2,1)S(1)}, f16[128,2048]{1,0:T(8,128)(2,1)S(1)}, u32[]{:S(2)}, u32[]{:S(2)}) collective-permute-start(f16[128,2048]{1,0:T(8,128)(2,1)S(1)} %get-tuple-element.145), channel_id=1, source_target_pairs={{0,16},{24,8},{1,17},{25,9},{10,26},{18,2},{11,27},{19,3},{12,28},... | collective-permute-start | bytes 1572872 | tf_op jit(solution)/shard_map/ppermute | solution.py:255
  91.5 1.4 add_convert_fusion
  92.9 4.5 %collective-permute-start.11 = (f16[128,2048]{1,0:T(8,128)(2,1)}, f16[128,2048]{1,0:T(8,128)(2,1)}, u32[]{:S(2)}, u32[]{:S(2)}) collective-permute-start(f16[128,2048]{1,0:T(8,128)(2,1)} %get-tuple-element.151), channel_id=1, source_target_pairs={{0,8},{24,16},{1,9},{25,17},{10,2},{18,26},{11,3},{19,27},{12,4},{... | collective-permute-start | bytes 1572872 | tf_op jit(solution)/shard_map/ppermute | solution.py:255
  97.4 2.1 %collective-permute-start.12 = (f16[128,2048]{1,0:T(8,128)(2,1)}, f16[128,2048]{1,0:T(8,128)(2,1)}, u32[]{:S(2)}, u32[]{:S(2)}) collective-permute-start(f16[128,2048]{1,0:T(8,128)(2,1)} %get-tuple-element.149), channel_id=1, source_target_pairs={{0,16},{24,8},{1,17},{25,9},{10,26},{18,2},{11,27},{19,3},{12,28},... | collective-permute-start | bytes 1572872 | tf_op jit(solution)/shard_map/ppermute | solution.py:255
  99.5 26.7 %collective-permute-done.16 = f16[128,2048]{1,0:T(8,128)(2,1)S(1)} collective-permute-done((f16[128,2048]{1,0:T(8,128)(2,1)S(1)}, f16[128,2048]{1,0:T(8,128)(2,1)S(1)}, u32[]{:S(2)}, u32[]{:S(2)}) %collective-permute-start.16) | collective-permute-done | bytes 524320 | tf_op jit(solution)/shard_map/ppermute | solution.py:255
  126.3 1.5 collective-permute-start.13
  127.7 1.3 collective-permute-start.21
  129.0 4.6 %collective-permute-start.8 = (f16[256,2048]{1,0:T(8,128)(2,1)}, f16[256,2048]{1,0:T(8,128)(2,1)}, u32[]{:S(2)}, u32[]{:S(2)}) collective-permute-start(f16[256,2048]{1,0:T(8,128)(2,1)} %add_convert_fusion), channel_id=1, source_target_pairs={{16,0},{17,1},{18,10},{19,11},{12,20},{13,21},{14,30},{15,31}} | collective-permute-start | bytes 3145736 | tf_op jit(solution)/shard_map/ppermute | solution.py:230
  133.6 3.2 %fusion.13 = f16[256,1024]{1,0:T(8,128)(2,1)} fusion(bf16[4096,256]{1,0:T(8,128)(2,1)S(1)} %join.7, bf16[4096,2048]{1,0:T(8,128)(2,1)S(1)} %lagged.1), kind=kOutput, calls=%fused_computation.39 | convolution fusion | flops 2148007936 | bytes 11010048 | tf_op jit(solution)/shard_map/dot_general | solution.py:193
  136.8 8.5 %collective-permute-done.21 = f16[256,1024]{1,0:T(8,128)(2,1)S(1)} collective-permute-done((f16[256,1024]{1,0:T(8,128)(2,1)S(1)}, f16[256,1024]{1,0:T(8,128)(2,1)S(1)}, u32[]{:S(2)}, u32[]{:S(2)}) %collective-permute-start.21) | collective-permute-done | bytes 524320 | tf_op jit(solution)/shard_map/ppermute | solution.py:225
  146.2 1.3 collective-permute-start.22
  147.5 2.2 %add_convert_fusion.2 = f16[256,1024]{1,0:T(8,128)(2,1)} fusion(f16[256,1024]{1,0:T(8,128)(2,1)} %copy-done.6, f16[256,1024]{1,0:T(8,128)(2,1)} %copy-done.5), kind=kLoop, calls=%fused_computation.46 | loop fusion | flops 1048576 | bytes 1572864 | tf_op jit(solution)/shard_map/convert_element_type | solution.py:263
  149.7 1.3 collective-permute-start.23
  151.0 11.2 %collective-permute-done.22 = f16[256,1024]{1,0:T(8,128)(2,1)} collective-permute-done((f16[256,1024]{1,0:T(8,128)(2,1)}, f16[256,1024]{1,0:T(8,128)(2,1)}, u32[]{:S(2)}, u32[]{:S(2)}) %collective-permute-start.22) | collective-permute-done | bytes 524320 | tf_op jit(solution)/shard_map/ppermute | solution.py:225
  162.2 3.1 %conditional.1 = ((f32[256,1024]{1,0:T(8,128)S(1)}, f32[256,1024]{1,0:T(8,128)})) conditional(s32[]{:T(128)} %clamp.3, (f16[256,2048]{1,0:T(8,128)(2,1)S(1)}, f16[256,2048]{1,0:T(8,128)(2,1)S(1)}, f16[256,2048]{1,0:T(8,128)(2,1)}) %tuple.27, (f16[128,2048]{1,0:T(8,128)(2,1)S(1)}, f16[128,2048]{1,0:T(8,128)(2,1)}, ...), branch_computations={%region_3.4_spmd, %region_4.5_spmd, %region_5.6_spmd, %region_6.7_... | conditional | flops 4194304 | bytes 10485784 | solution.py:287
  162.2 1.9 convert_add_fusion.13
  164.1 1.0 pad_maximum_fusion.7
  165.3 17.2 %collective-permute-start.28 = (f32[256,1024]{1,0:T(8,128)}, f32[256,1024]{1,0:T(8,128)S(1)}, u32[]{:S(2)}, u32[]{:S(2)}) collective-permute-start(f32[256,1024]{1,0:T(8,128)} %get-tuple-element.114), channel_id=1, source_target_pairs={{0,1},{1,0},{2,3},{3,2},{4,5},{5,4},{6,7},{7,6},{8,9},{9,8},{10,11... | collective-permute-start | bytes 3145736 | tf_op jit(solution)/shard_map/ppermute | solution.py:288
  182.5 2.2 %add_convert_fusion.1 = f16[256,1024]{1,0:T(8,128)(2,1)} fusion(f16[256,1024]{1,0:T(8,128)(2,1)} %collective-permute-done.22, f16[256,1024]{1,0:T(8,128)(2,1)} %fusion.13), kind=kLoop, calls=%fused_computation.43 | loop fusion | flops 1048576 | bytes 1572864 | tf_op jit(solution)/shard_map/convert_element_type | solution.py:263
  184.7 1.3 collective-permute-start.29
  186.0 1.2 add_bitcast_fusion.1
  188.1 12.4 %collective-permute-done.29 = f16[256,1024]{1,0:T(8,128)(2,1)} collective-permute-done((f16[256,1024]{1,0:T(8,128)(2,1)}, f16[256,1024]{1,0:T(8,128)(2,1)}, u32[]{:S(2)}, u32[]{:S(2)}) %collective-permute-start.29) | collective-permute-done | bytes 524320 | tf_op jit(solution)/shard_map/ppermute | solution.py:264
  200.5 1.2 add_bitcast_fusion
  202.1 1.2 multiply_dynamic-update-slice_fusion
  (71 shorter events, 9.3 us)
Async XLA Ops:
  0.0 7.9 %copy-start = (f32[4096,256]{1,0:T(8,128)S(1)}, f32[4096,256]{1,0:T(8,128)}, u32[]{:S(2)}) copy-start(f32[4096,256]{1,0:T(8,128)} %param.6) | copy-start | bytes 12582916
  2.9 3.8 %collective-permute-start = (f32[3,256]{1,0:T(4,128)S(1)}, f32[3,256]{1,0:T(4,128)S(1)}, u32[]{:S(2)}, u32[]{:S(2)}) collective-permute-start(f32[3,256]{1,0:T(4,128)S(1)} %pad_maximum_fusion.8), channel_id=1, source_target_pairs={{0,8},{8,16},{16,24},{24,0},{1,9},{9,17},{17,25},{25,1},{2,10},{10... | collective-permute-start | bytes 9224 | tf_op jit(solution)/shard_map/ppermute | solution.py:151
  4.3 3.4 %collective-permute-start.1 = (f32[3,256]{1,0:T(4,128)S(1)}, f32[3,256]{1,0:T(4,128)S(1)}, u32[]{:S(2)}, u32[]{:S(2)}) collective-permute-start(f32[3,256]{1,0:T(4,128)S(1)} %pad_maximum_fusion.8), channel_id=1, source_target_pairs={{0,16},{8,24},{16,0},{24,8},{1,17},{9,25},{17,1},{25,9},{2,18},{10... | collective-permute-start | bytes 9224 | tf_op jit(solution)/shard_map/ppermute | solution.py:151
  5.4 2.5 %collective-permute-start.2 = (f32[3,256]{1,0:T(4,128)S(1)}, f32[3,256]{1,0:T(4,128)S(1)}, u32[]{:S(2)}, u32[]{:S(2)}) collective-permute-start(f32[3,256]{1,0:T(4,128)S(1)} %pad_maximum_fusion.8), channel_id=1, source_target_pairs={{0,24},{8,0},{16,8},{24,16},{1,25},{9,1},{17,9},{25,17},{2,26},{10... | collective-permute-start | bytes 9224 | tf_op jit(solution)/shard_map/ppermute | solution.py:151
  8.4 22.6 %collective-permute-start.14 = (bf16[4096,128]{1,0:T(8,128)(2,1)S(1)}, bf16[4096,128]{1,0:T(8,128)(2,1)}, u32[]{:S(2)}, u32[]{:S(2)}) collective-permute-start(bf16[4096,128]{1,0:T(8,128)(2,1)S(1)} %multiply_convert_fusion.right_ref.refs_3_.refs_4_), channel_id=1, source_target_pairs={{0,2},{1,3},{2,0},{3,1},{4,6},{5,7},{6,4},{7,5},{8,10},{9,11},{10,... | collective-permute-start | bytes 3145736 | tf_op jit(solution)/shard_map/ppermute | solution.py:176
  9.7 22.3 %collective-permute-start.15 = (bf16[4096,128]{1,0:T(8,128)(2,1)S(1)}, bf16[4096,128]{1,0:T(8,128)(2,1)}, u32[]{:S(2)}, u32[]{:S(2)}) collective-permute-start(bf16[4096,128]{1,0:T(8,128)(2,1)S(1)} %multiply_convert_fusion.1.left_ref.refs_1_.refs_2_), channel_id=1, source_target_pairs={{0,4},{1,5},{2,6},{3,7},{4,0},{5,1},{6,2},{7,3},{8,12},{9,13},{10,... | collective-permute-start | bytes 3145736 | tf_op jit(solution)/shard_map/ppermute | solution.py:176
  9.9 25.4 %collective-permute-start.6 = (bf16[4096,128]{1,0:T(8,128)(2,1)S(1)}, bf16[4096,128]{1,0:T(8,128)(2,1)S(1)}, u32[]{:S(2)}, u32[]{:S(2)}) collective-permute-start(bf16[4096,128]{1,0:T(8,128)(2,1)S(1)} %multiply_convert_fusion.right_ref.refs_3_.refs_4_), channel_id=1, source_target_pairs={{0,1},{1,0},{2,3},{3,2},{4,5},{5,4},{6,7},{7,6},{8,9},{9,8},{10,11... | collective-permute-start | bytes 3145736 | tf_op jit(solution)/shard_map/ppermute | solution.py:178
  12.7 23.6 %collective-permute-start.5 = (bf16[4096,128]{1,0:T(8,128)(2,1)S(1)}, bf16[4096,128]{1,0:T(8,128)(2,1)}, u32[]{:S(2)}, u32[]{:S(2)}) collective-permute-start(bf16[4096,128]{1,0:T(8,128)(2,1)S(1)} %multiply_convert_fusion.1.left_ref.refs_1_.refs_2_), channel_id=1, source_target_pairs={{0,1},{1,0},{2,3},{3,2},{4,5},{5,4},{6,7},{7,6},{8,9},{9,8},{10,11... | collective-permute-start | bytes 3145736 | tf_op jit(solution)/shard_map/ppermute | solution.py:178
  12.7 3.9 %collective-permute-start.24 = (f32[1,256]{1,0:T(1,128)S(1)}, f32[1,256]{1,0:T(1,128)S(1)}, u32[]{:S(2)}, u32[]{:S(2)}) collective-permute-start(f32[1,256]{1,0:T(1,128)S(1)} %get-tuple-element.152), channel_id=1, source_target_pairs={{0,1},{1,0},{2,3},{3,2},{4,5},{5,4},{6,7},{7,6},{8,9},{9,8},{10,11... | collective-permute-start | bytes 3080 | tf_op jit(solution)/shard_map/ppermute | solution.py:186
  16.7 4.9 %collective-permute-start.3 = (f32[16,256]{1,0:T(8,128)S(1)}, f32[16,256]{1,0:T(8,128)S(1)}, u32[]{:S(2)}, u32[]{:S(2)}) collective-permute-start(f32[16,256]{1,0:T(8,128)S(1)} %slice.277), channel_id=1, source_target_pairs={{0,8},{8,16},{16,24},{1,9},{9,17},{17,25},{2,10},{10,18},{18,26},{... | collective-permute-start | bytes 49160 | tf_op jit(solution)/shard_map/ppermute | solution.py:180
  21.5 12.5 %collective-permute-start.4 = (bf16[16,256]{1,0:T(8,128)(2,1)S(1)}, bf16[16,256]{1,0:T(8,128)(2,1)S(1)}, u32[]{:S(2)}, u32[]{:S(2)}) collective-permute-start(bf16[16,256]{1,0:T(8,128)(2,1)S(1)} %fusion.19.refs_0_), channel_id=1, source_target_pairs={{0,1},{1,0},{2,3},{3,2},{4,5},{5,4},{6,7},{7,6},{8,9},{9,8},{10,11... | collective-permute-start | bytes 24584 | tf_op jit(solution)/shard_map/ppermute | solution.py:183
  31.1 23.9 %collective-permute-start.10 = (bf16[4096,128]{1,0:T(8,128)(2,1)S(1)}, bf16[4096,128]{1,0:T(8,128)(2,1)S(1)}, u32[]{:S(2)}, u32[]{:S(2)}) collective-permute-start(bf16[4096,128]{1,0:T(8,128)(2,1)S(1)} %multiply_convert_fusion.right_ref.refs_3_.refs_4_), channel_id=1, source_target_pairs={{0,4},{1,5},{2,6},{3,7},{4,0},{5,1},{6,2},{7,3},{8,12},{9,13},{10,... | collective-permute-start | bytes 3145736 | tf_op jit(solution)/shard_map/ppermute | solution.py:176
  32.0 22.9 %collective-permute-start.9 = (bf16[4096,128]{1,0:T(8,128)(2,1)S(1)}, bf16[4096,128]{1,0:T(8,128)(2,1)S(1)}, u32[]{:S(2)}, u32[]{:S(2)}) collective-permute-start(bf16[4096,128]{1,0:T(8,128)(2,1)S(1)} %multiply_convert_fusion.1.left_ref.refs_1_.refs_2_), channel_id=1, source_target_pairs={{0,2},{1,3},{2,0},{3,1},{4,6},{5,7},{6,4},{7,5},{8,10},{9,11},{10,... | collective-permute-start | bytes 3145736 | tf_op jit(solution)/shard_map/ppermute | solution.py:176
  34.1 54.1 %collective-permute-start.25 = (f32[2,256]{1,0:T(2,128)S(1)}, f32[2,256]{1,0:T(2,128)S(1)}, u32[]{:S(2)}, u32[]{:S(2)}) collective-permute-start(f32[2,256]{1,0:T(2,128)S(1)} %pad_maximum_fusion.9), channel_id=1, source_target_pairs={{0,6},{1,7},{2,4},{3,5},{4,2},{5,3},{6,0},{7,1},{8,14},{9,15},{10,... | collective-permute-start | bytes 6152 | tf_op jit(solution)/shard_map/ppermute | solution.py:190
  35.4 57.6 %collective-permute-start.26 = (f32[2,256]{1,0:T(2,128)S(1)}, f32[2,256]{1,0:T(2,128)S(1)}, u32[]{:S(2)}, u32[]{:S(2)}) collective-permute-start(f32[2,256]{1,0:T(2,128)S(1)} %pad_maximum_fusion.9), channel_id=1, source_target_pairs={{0,4},{1,5},{2,6},{3,7},{4,0},{5,1},{6,2},{7,3},{8,12},{9,13},{10,... | collective-permute-start | bytes 6152 | tf_op jit(solution)/shard_map/ppermute | solution.py:190
  59.8 21.9 %collective-permute-start.20 = (bf16[4096,128]{1,0:T(8,128)(2,1)S(1)}, bf16[4096,128]{1,0:T(8,128)(2,1)S(1)}, u32[]{:S(2)}, u32[]{:S(2)}) collective-permute-start(bf16[4096,128]{1,0:T(8,128)(2,1)S(1)} %collective-permute-done.10.right_ref), channel_id=1, source_target_pairs={{0,2},{1,3},{2,0},{3,1},{4,6},{5,7},{6,4},{7,5},{8,10},{9,11},{10,... | collective-permute-start | bytes 3145736 | tf_op jit(solution)/shard_map/ppermute | solution.py:237
  59.9 21.8 %collective-permute-start.19 = (bf16[4096,128]{1,0:T(8,128)(2,1)S(1)}, bf16[4096,128]{1,0:T(8,128)(2,1)S(1)}, u32[]{:S(2)}, u32[]{:S(2)}) collective-permute-start(bf16[4096,128]{1,0:T(8,128)(2,1)S(1)} %collective-permute-done.9.left_ref), channel_id=1, source_target_pairs={{0,4},{1,5},{2,6},{3,7},{4,0},{5,1},{6,2},{7,3},{8,12},{9,13},{10,... | collective-permute-start | bytes 3145736 | tf_op jit(solution)/shard_map/ppermute | solution.py:237
  64.7 26.1 %collective-permute-start.7 = (f16[256,2048]{1,0:T(8,128)(2,1)S(1)}, f16[256,2048]{1,0:T(8,128)(2,1)S(1)}, u32[]{:S(2)}, u32[]{:S(2)}) collective-permute-start(f16[256,2048]{1,0:T(8,128)(2,1)S(1)} %fusion.4), channel_id=1, source_target_pairs={{8,0},{24,16},{9,1},{25,17},{2,10},{26,18},{3,11},{27,19},{4,12},{... | collective-permute-start | bytes 3145736 | tf_op jit(solution)/shard_map/ppermute | solution.py:225
  81.7 15.7 %collective-permute-start.27 = (f32[2,256]{1,0:T(2,128)S(1)}, f32[2,256]{1,0:T(2,128)S(1)}, u32[]{:S(2)}, u32[]{:S(2)}) collective-permute-start(f32[2,256]{1,0:T(2,128)S(1)} %pad_maximum_fusion.9), channel_id=1, source_target_pairs={{0,2},{1,3},{2,0},{3,1},{4,6},{5,7},{6,4},{7,5},{8,10},{9,11},{10,... | collective-permute-start | bytes 6152 | tf_op jit(solution)/shard_map/ppermute | solution.py:190
  81.7 44.5 %collective-permute-start.16 = (f16[128,2048]{1,0:T(8,128)(2,1)S(1)}, f16[128,2048]{1,0:T(8,128)(2,1)S(1)}, u32[]{:S(2)}, u32[]{:S(2)}) collective-permute-start(f16[128,2048]{1,0:T(8,128)(2,1)S(1)} %get-tuple-element.147), channel_id=1, source_target_pairs={{0,8},{24,16},{1,9},{25,17},{10,2},{18,26},{11,3},{19,27},{12,4},{... | collective-permute-start | bytes 1572872 | tf_op jit(solution)/shard_map/ppermute | solution.py:255
  88.1 48.7 %copy-start.5 = (f16[256,1024]{1,0:T(8,128)(2,1)}, f16[256,1024]{1,0:T(8,128)(2,1)S(1)}, u32[]{:S(2)}) copy-start(f16[256,1024]{1,0:T(8,128)(2,1)S(1)} %fusion.16) | copy-start | bytes 1572868
  88.2 39.6 %collective-permute-start.17 = (f16[128,2048]{1,0:T(8,128)(2,1)S(1)}, f16[128,2048]{1,0:T(8,128)(2,1)S(1)}, u32[]{:S(2)}, u32[]{:S(2)}) collective-permute-start(f16[128,2048]{1,0:T(8,128)(2,1)S(1)} %get-tuple-element.145), channel_id=1, source_target_pairs={{0,16},{24,8},{1,17},{25,9},{10,26},{18,2},{11,27},{19,3},{12,28},... | collective-permute-start | bytes 1572872 | tf_op jit(solution)/shard_map/ppermute | solution.py:255
  90.8 38.2 %collective-permute-start.18 = (f16[128,2048]{1,0:T(8,128)(2,1)S(1)}, f16[128,2048]{1,0:T(8,128)(2,1)S(1)}, u32[]{:S(2)}, u32[]{:S(2)}) collective-permute-start(f16[128,2048]{1,0:T(8,128)(2,1)S(1)} %get-tuple-element.144), channel_id=1, source_target_pairs={{8,16},{16,8},{9,17},{17,9},{2,26},{26,2},{3,27},{27,3},{4,28},{28... | collective-permute-start | bytes 1572872 | tf_op jit(solution)/shard_map/ppermute | solution.py:255
  92.9 56.7 %collective-permute-start.11 = (f16[128,2048]{1,0:T(8,128)(2,1)}, f16[128,2048]{1,0:T(8,128)(2,1)}, u32[]{:S(2)}, u32[]{:S(2)}) collective-permute-start(f16[128,2048]{1,0:T(8,128)(2,1)} %get-tuple-element.151), channel_id=1, source_target_pairs={{0,8},{24,16},{1,9},{25,17},{10,2},{18,26},{11,3},{19,27},{12,4},{... | collective-permute-start | bytes 1572872 | tf_op jit(solution)/shard_map/ppermute | solution.py:255
  97.4 53.6 %collective-permute-start.12 = (f16[128,2048]{1,0:T(8,128)(2,1)}, f16[128,2048]{1,0:T(8,128)(2,1)}, u32[]{:S(2)}, u32[]{:S(2)}) collective-permute-start(f16[128,2048]{1,0:T(8,128)(2,1)} %get-tuple-element.149), channel_id=1, source_target_pairs={{0,16},{24,8},{1,17},{25,9},{10,26},{18,2},{11,27},{19,3},{12,28},... | collective-permute-start | bytes 1572872 | tf_op jit(solution)/shard_map/ppermute | solution.py:255
  126.2 10.6 %copy-start.1 = (f16[128,2048]{1,0:T(8,128)(2,1)}, f16[128,2048]{1,0:T(8,128)(2,1)S(1)}, u32[]{:S(2)}) copy-start(f16[128,2048]{1,0:T(8,128)(2,1)S(1)} %collective-permute-done.16) | copy-start | bytes 1572868
  126.3 24.7 %collective-permute-start.13 = (f16[128,2048]{1,0:T(8,128)(2,1)}, f16[128,2048]{1,0:T(8,128)(2,1)}, u32[]{:S(2)}, u32[]{:S(2)}) collective-permute-start(f16[128,2048]{1,0:T(8,128)(2,1)} %get-tuple-element.148), channel_id=1, source_target_pairs={{8,16},{16,8},{9,17},{17,9},{2,26},{26,2},{3,27},{27,3},{4,28},{28... | collective-permute-start | bytes 1572872 | tf_op jit(solution)/shard_map/ppermute | solution.py:255
  127.7 9.1 %copy-start.2 = (f16[128,2048]{1,0:T(8,128)(2,1)}, f16[128,2048]{1,0:T(8,128)(2,1)S(1)}, u32[]{:S(2)}) copy-start(f16[128,2048]{1,0:T(8,128)(2,1)S(1)} %collective-permute-done.17) | copy-start | bytes 1572868
  127.7 17.6 %collective-permute-start.21 = (f16[256,1024]{1,0:T(8,128)(2,1)S(1)}, f16[256,1024]{1,0:T(8,128)(2,1)S(1)}, u32[]{:S(2)}, u32[]{:S(2)}) collective-permute-start(f16[256,1024]{1,0:T(8,128)(2,1)S(1)} %fusion.16), channel_id=1, source_target_pairs={{0,8},{16,24},{1,9},{17,25},{2,10},{26,18},{3,11},{27,19},{4,12},{... | collective-permute-start | bytes 1572872 | tf_op jit(solution)/shard_map/ppermute | solution.py:225
  129.0 7.8 %copy-start.3 = (f16[128,2048]{1,0:T(8,128)(2,1)}, f16[128,2048]{1,0:T(8,128)(2,1)S(1)}, u32[]{:S(2)}) copy-start(f16[128,2048]{1,0:T(8,128)(2,1)S(1)} %collective-permute-done.18) | copy-start | bytes 1572868
  129.0 33.2 %collective-permute-start.8 = (f16[256,2048]{1,0:T(8,128)(2,1)}, f16[256,2048]{1,0:T(8,128)(2,1)}, u32[]{:S(2)}, u32[]{:S(2)}) collective-permute-start(f16[256,2048]{1,0:T(8,128)(2,1)} %add_convert_fusion), channel_id=1, source_target_pairs={{16,0},{17,1},{18,10},{19,11},{12,20},{13,21},{14,30},{15,31}} | collective-permute-start | bytes 3145736 | tf_op jit(solution)/shard_map/ppermute | solution.py:230
  145.3 0.8 copy-start.6
  146.2 16.0 %collective-permute-start.22 = (f16[256,1024]{1,0:T(8,128)(2,1)}, f16[256,1024]{1,0:T(8,128)(2,1)}, u32[]{:S(2)}, u32[]{:S(2)}) collective-permute-start(f16[256,1024]{1,0:T(8,128)(2,1)} %fusion.13), channel_id=1, source_target_pairs={{0,8},{16,24},{1,9},{17,25},{2,10},{26,18},{3,11},{27,19},{4,12},{... | collective-permute-start | bytes 1572872 | tf_op jit(solution)/shard_map/ppermute | solution.py:225
  149.7 36.3 %collective-permute-start.23 = (f16[256,1024]{1,0:T(8,128)(2,1)}, f16[256,1024]{1,0:T(8,128)(2,1)}, u32[]{:S(2)}, u32[]{:S(2)}) collective-permute-start(f16[256,1024]{1,0:T(8,128)(2,1)} %add_convert_fusion.2), channel_id=1, source_target_pairs={{8,24},{9,25},{10,18},{11,19},{20,12},{21,13},{22,6},{23,7}} | collective-permute-start | bytes 1572872 | tf_op jit(solution)/shard_map/ppermute | solution.py:264
  165.3 35.2 %collective-permute-start.28 = (f32[256,1024]{1,0:T(8,128)}, f32[256,1024]{1,0:T(8,128)S(1)}, u32[]{:S(2)}, u32[]{:S(2)}) collective-permute-start(f32[256,1024]{1,0:T(8,128)} %get-tuple-element.114), channel_id=1, source_target_pairs={{0,1},{1,0},{2,3},{3,2},{4,5},{5,4},{6,7},{7,6},{8,9},{9,8},{10,11... | collective-permute-start | bytes 3145736 | tf_op jit(solution)/shard_map/ppermute | solution.py:288
  184.7 15.8 %collective-permute-start.29 = (f16[256,1024]{1,0:T(8,128)(2,1)}, f16[256,1024]{1,0:T(8,128)(2,1)}, u32[]{:S(2)}, u32[]{:S(2)}) collective-permute-start(f16[256,1024]{1,0:T(8,128)(2,1)} %add_convert_fusion.1), channel_id=1, source_target_pairs={{8,25},{9,24},{10,19},{11,18},{20,13},{21,12},{22,7},{23,6}} | collective-permute-start | bytes 1572872 | tf_op jit(solution)/shard_map/ppermute | solution.py:264
  187.3 0.7 copy-start.7
  188.1 12.4 %copy-start.4 = (f32[4,256,512]{2,1,0:T(8,128)}, f32[4,256,512]{2,1,0:T(8,128)S(1)}, u32[]{:S(2)}) copy-start(f32[4,256,512]{2,1,0:T(8,128)S(1)} %multiply_dynamic-update-slice_fusion.1) | copy-start | bytes 6291460
